TPU v7x, 256 devices: a whole 4x4x8 slice. The times are simulated.
256 devices in a mesh: sta: 8 (over x, y_lo), tm: 32 (over z, y_hi, core).
Axes of the slice: x: 4, y: 4 (y_hi: 2, y_lo: 2; y = y_hi * 2 + y_lo), z: 8, core: 2. Of those that a mesh axis runs over, the one named last changes fastest.
Arguments:
- record: bfloat16 [16, 3, 16384], P('sta', None, 'tm'), may hold values from -6 to 6
- templates: bfloat16 [16, 256, 768], P('sta'), may hold values from -6 to 6
- moveouts: int32 [16, 256], P('sta'), may hold values from 0 to 255
- live_mask: int32 [16], P('sta'), may hold values 0 or 1
- owner_order: int32 [256], replicated, may hold values from 0 to 255, each once
Outputs:
- detection: float32 [256, 16384], P('sta', 'tm')
All inputs are finite; a program needn't handle non-finite values. No bound on the sum of `live_mask` on one device may be relied on, other than what follows from the above.
Results may differ from a plain program's by a relative error of at most 0.0029.
Values may be sent and summed in bfloat16 or wider, within the bound.
No kernel may reach another device: no remote copies, remote signals or barrier semaphores. Data moves between devices by JAX's collectives and lax.ppermute only.
A program may use at most 64 MiB of HBM per device.

v0:
```python
import math

import jax
import jax.numpy as jnp
from jax import lax
from jax.sharding import PartitionSpec as P

TLEN = 256
MAXM = 256


epsilon = 1e-05


def passed_along(value, axis, steps):
    count = lax.axis_size(axis)
    initial, last = (max(0, -steps), min(count, count - steps))
    return lax.ppermute(value, axis, [(source, source + steps) for source in range(initial, last)])


def toeplitz(signal, span, width):
    components = signal.shape[0]
    length = width + span
    tiled = jnp.tile(signal, (1, span + 1))
    flat = tiled[:, : span * (length + 1)]
    return flat.reshape(components, span, length + 1)[:, :, :width]


def normalize_block(extended, templates, columns):
    components = extended.shape[1]

    def one_station(items):
        record_one, template_one = items
        squares = jnp.sum(jnp.square(record_one.astype(jnp.float32)), axis=0)
        running = jnp.concatenate([jnp.zeros((1,), jnp.float32), jnp.cumsum(squares)])
        energy = running[TLEN : TLEN + columns] - running[:columns]
        record_rms = jnp.sqrt(energy / (components * TLEN) + epsilon)
        template_rms = jnp.sqrt(
            jnp.mean(jnp.square(template_one.astype(jnp.float32)), axis=-1) + epsilon
        )
        frames = toeplitz(record_one, TLEN, columns).reshape(components * TLEN, columns)
        correlation = jnp.dot(template_one, frames, preferred_element_type=jnp.float32)
        scaled = correlation / (components * TLEN * record_rms[None, :] * template_rms[:, None])
        return scaled.astype(jnp.bfloat16)

    return lax.map(one_station, (extended, templates))


def shift_rows(values, shifts, width):
    current = values
    for bit_place in reversed(range((MAXM - 1).bit_length())):
        step_size = 1 << bit_place
        new_len = current.shape[-1] - step_size
        taken = shifts >> bit_place & 1 == 1
        current = jnp.where(
            taken[..., None], current[..., step_size : step_size + new_len], current[..., :new_len]
        )
    return current[..., :width]


def shards(record, templates, moveouts, live_mask, owner_order):
    stations = record.shape[0]
    components = record.shape[1]
    block_len = record.shape[2]
    kcount = templates.shape[1]
    next_rim = passed_along(record[:, :, :TLEN], "tm", -1)
    extended = jnp.concatenate([record, next_rim], axis=2)
    own_scores = normalize_block(extended, templates, block_len)
    borrowed = passed_along(own_scores[:, :, :MAXM], "tm", -1)
    scores = jnp.concatenate([own_scores, borrowed], axis=2)
    stack_scale = math.sqrt(components * TLEN / (stations * lax.axis_size("sta")))
    weights = live_mask.astype(jnp.float32) * stack_scale
    own_rows = kcount // lax.axis_size("sta")
    chosen_scores = jnp.take(scores, owner_order, axis=1)
    shifts = jnp.take(moveouts, owner_order, axis=1)
    picked = shift_rows(chosen_scores, shifts, block_len)
    summed = lax.psum(jnp.sum(picked.astype(jnp.float32) * weights[:, None, None], axis=0), "sta")
    return lax.dynamic_slice_in_dim(summed, lax.axis_index("sta") * own_rows, own_rows, 0)


def solution(mesh):
    placed = (P("sta", None, "tm"), P("sta", None, None), P("sta", None), P("sta"), P())
    return jax.shard_map(
        shards, mesh=mesh, in_specs=placed, out_specs=P("sta", "tm"), check_vma=False
    )
```

profile of v0, /device:TPU:32, one launch (start us, length us, event | category | flops | bytes accessed | tf_op | source)
XLA Modules:
  0.0 152.0 jit_solution(10830028386999631244)
XLA Ops:
  6.5 0.7 copy.33
  7.2 4.1 %collective-permute-start = (bf16[2,3,256]{2,1,0:T(4,128)(2,1)S(1)}, bf16[2,3,256]{2,1,0:T(4,128)(2,1)S(1)}, u32[]{:S(2)}, u32[]{:S(2)}) collective-permute-start(bf16[2,3,256]{2,1,0:T(4,128)(2,1)S(1)} %slice.101), channel_id=1, source_target_pairs={{1,0},{2,1},{3,2},{4,3},{5,4},{6,5},{7,6},{8,7},{9,8},{10,9},{11,1... | collective-permute-start | bytes 9224 | tf_op jit(solution)/shard_map/ppermute | solution.py:18
  11.3 0.7 compare_select_fusion
  12.0 0.7 compare_and_fusion
  12.7 0.8 copy.22
  13.5 0.7 gather_fusion
  14.3 0.1 copy.23
  14.4 16.3 %while.10 = (s32[]{:T(128)}, bf16[2,256,512]{2,1,0:T(8,128)(2,1)}, bf16[2,256,768]{2,1,0:T(8,128)(2,1)}, bf16[2,3,768]{2,1,0:T(4,128)(2,1)S(1)}, s32[]{:T(128)}, /*index=5*/f32[]{:T(128)}, f32[1]{0:T(128)}) while((s32[]{:T(128)}, bf16[2,256,512]{2,1,0:T(8,128)(2,1)}, bf16[2,256,768]{2,1,0:T(8,128)(2,1)}, bf16[2,3,768]{2,1,0:T(4,128)(2,1)S(1)}, ...), condition=%wide.region_5.6_spmd, body=%wide.region_0.5_spmd.sunk | while | flops 202417184 | bytes 21436772 | solution.py:46
  14.4 0.3 reduce-window.13
  14.7 0.1 slice.153
  14.8 0.1 slice_reduce_fusion.2
  14.9 0.1 add_bitcast_fusion.2
  15.0 0.1 pad_maximum_fusion.4
  15.1 0.1 sqrt_multiply_fusion.2
  15.2 0.1 broadcast_bitcast_fusion.2
  15.2 0.6 copy.38
  15.9 0.6 slice.151
  16.5 1.0 reshape.175
  17.5 2.8 %reshape.176 = bf16[3,256,769]{2,1,0:T(8,128)(2,1)S(1)} reshape(bf16[590592]{0:T(1024)(128)(2,1)S(1)} %reshape.175) | data formatting | bytes 2362368 | tf_op jit(solution)/shard_map/while/body/eval_jaxpr/reshape | solution.py:26
  20.4 0.2 multiply_reduce_fusion.6
  20.6 0.8 copy-done.1
  21.4 0.4 fusion.14
  21.7 0.8 copy-done.2
  22.5 0.3 reduce-window.13
  22.8 0.1 slice.153
  22.9 0.1 slice_reduce_fusion.2
  23.0 0.1 add_bitcast_fusion.2
  23.1 0.1 pad_maximum_fusion.4
  23.2 0.1 sqrt_multiply_fusion.2
  23.3 0.1 broadcast_bitcast_fusion.2
  23.4 0.6 copy.38
  24.0 0.6 slice.151
  24.6 1.0 reshape.175
  25.6 2.8 %reshape.176 = bf16[3,256,769]{2,1,0:T(8,128)(2,1)S(1)} reshape(bf16[590592]{0:T(1024)(128)(2,1)S(1)} %reshape.175) | data formatting | bytes 2362368 | tf_op jit(solution)/shard_map/while/body/eval_jaxpr/reshape | solution.py:26
  28.5 0.2 multiply_reduce_fusion.6
  28.7 0.8 copy-done.1
  29.5 0.4 fusion.14
  29.9 0.8 copy-done.2
  30.7 1.6 %copy.35 = bf16[2,256,512]{2,0,1:T(2,128)(2,1)S(1)} copy(bf16[2,256,512]{2,1,0:T(8,128)(2,1)} %get-tuple-element.27) | data formatting | bytes 1048576 | tf_op jit(solution)/shard_map/while | solution.py:46
  32.2 0.2 slice.102
  32.4 4.5 %collective-permute-start.1 = (bf16[2,256,256]{2,0,1:T(2,128)(2,1)S(1)}, bf16[2,256,256]{2,0,1:T(2,128)(2,1)S(1)}, u32[]{:S(2)}, u32[]{:S(2)}) collective-permute-start(bf16[2,256,256]{2,0,1:T(2,128)(2,1)S(1)} %slice.102), channel_id=1, source_target_pairs={{1,0},{2,1},{3,2},{4,3},{5,4},{6,5},{7,6},{8,7},{9,8},{10,9},{11,1... | collective-permute-start | bytes 786440 | tf_op jit(solution)/shard_map/ppermute | solution.py:18
  36.9 0.2 copy.31
  37.1 0.2 copy.30
  37.3 0.2 copy.29
  37.5 0.2 copy.28
  37.7 0.2 copy.27
  37.9 0.2 copy.26
  38.1 0.2 copy.25
  38.2 0.2 copy.24
  38.4 2.2 %collective-permute-done.1 = bf16[2,256,256]{2,0,1:T(2,128)(2,1)S(1)} collective-permute-done((bf16[2,256,256]{2,0,1:T(2,128)(2,1)S(1)}, bf16[2,256,256]{2,0,1:T(2,128)(2,1)S(1)}, u32[]{:S(2)}, u32[]{:S(2)}) %collective-permute-start.1) | collective-permute-done | bytes 262176 | tf_op jit(solution)/shard_map/ppermute | solution.py:18
  40.6 0.7 pad_maximum_fusion.1
  41.3 2.3 %gather_fusion.1 = bf16[256,2,768]{2,1,0:T(2,128)(2,1)S(1)} fusion(bf16[2,256,768]{2,0,1:T(2,128)(2,1)S(1)} %pad_maximum_fusion.1, s32[1024]{0:T(1024)S(1)} %pad_clamp_fusion), kind=kCustom, calls=%fused_computation.1 | custom fusion | bytes 1573888 | tf_op jit(solution)/shard_map/jit(_take)/gather | solution.py:74
  43.6 1.3 fusion.6
  44.9 1.1 broadcast_select_fusion.1
  46.0 1.5 broadcast_select_fusion.2
  47.5 1.5 broadcast_select_fusion.3
  49.0 1.5 broadcast_select_fusion.4
  50.5 1.5 broadcast_select_fusion.5
  52.0 1.5 broadcast_select_fusion.6
  53.6 1.5 broadcast_select_fusion.7
  55.1 1.7 %fusion.7 = (bf16[2,256,513]{2,0,1:T(2,128)(2,1)S(1)}, bf16[2,256,513]{2,0,1:T(2,128)(2,1)S(1)}) fusion(bf16[2,256,514]{2,0,1:T(2,128)(2,1)S(1)} %broadcast_select_fusion.7), kind=kLoop, calls=%fused_computation.45 | loop fusion | bytes 2101248 | tf_op jit(solution)/shard_map/slice | solution.py:56
  56.8 2.7 %multiply_reduce_fusion.2 = f32[256,512]{1,0:T(8,128)} fusion(f32[2]{0:T(128)S(1)} %convert_multiply_fusion, pred[2,256]{0,1:T(8,128)(4,1)S(1)} %copy.24, bf16[2,256,513]{2,0,1:T(2,128)(2,1)S(1)} %get-tuple-element.39, bf16[2,256,513]{2,0,1:T(2,128)(2,1)S(1)} %get-tuple-element.38), kind=kLoop, calls=%fused_computation.26 | loop fusion | flops 917504 | bytes 1573384 | tf_op jit(solution)/shard_map/reduce_sum | solution.py:77
  59.5 84.2 %all-reduce.2.cloned.1.call-done = f32[256,512]{1,0:T(8,128)} async-done(((f32[256,512]{1,0:T(8,128)}), f32[256,512]{1,0:T(8,128)}) %all-reduce.2.cloned.1.call-update) | async-done | bytes 524304 | tf_op jit(solution)/shard_map/psum | solution.py:77
  143.7 1.5 constant_dynamic-slice_fusion
  (27 shorter events, 0.3 us)
Async XLA Ops:
  6.5 137.1 %all-reduce.2.cloned.1.call-start = ((), (), s32[]{:S(2)}) async-start(), calls=%async_computation | async-start | bytes 1048576 | tf_op jit(solution)/shard_map/psum | solution.py:77
  7.2 7.1 %collective-permute-start = (bf16[2,3,256]{2,1,0:T(4,128)(2,1)S(1)}, bf16[2,3,256]{2,1,0:T(4,128)(2,1)S(1)}, u32[]{:S(2)}, u32[]{:S(2)}) collective-permute-start(bf16[2,3,256]{2,1,0:T(4,128)(2,1)S(1)} %slice.101), channel_id=1, source_target_pairs={{1,0},{2,1},{3,2},{4,3},{5,4},{6,5},{7,6},{8,7},{9,8},{10,9},{11,1... | collective-permute-start | bytes 9224 | tf_op jit(solution)/shard_map/ppermute | solution.py:18
  17.5 2.9 %copy-start = (bf16[2,256,768]{2,1,0:T(8,128)(2,1)S(1)}, bf16[2,256,768]{2,1,0:T(8,128)(2,1)}, u32[]{:S(2)}) copy-start(bf16[2,256,768]{2,1,0:T(8,128)(2,1)} %get-tuple-element.93) | copy-start | bytes 2359300 | tf_op jit(solution)/shard_map/while
  20.3 1.0 copy-start.1
  21.7 0.8 copy-start.2
  25.6 2.9 %copy-start = (bf16[2,256,768]{2,1,0:T(8,128)(2,1)S(1)}, bf16[2,256,768]{2,1,0:T(8,128)(2,1)}, u32[]{:S(2)}) copy-start(bf16[2,256,768]{2,1,0:T(8,128)(2,1)} %get-tuple-element.93) | copy-start | bytes 2359300 | tf_op jit(solution)/shard_map/while
  28.4 1.0 copy-start.1
  29.9 0.8 copy-start.2
  30.6 7.8 %copy-start.3 = (s32[2]{0:T(128)S(1)}, s32[2]{0:T(128)}, u32[]{:S(2)}) copy-start(s32[2]{0:T(128)} %param.10) | copy-start | bytes 28
  32.4 8.2 %collective-permute-start.1 = (bf16[2,256,256]{2,0,1:T(2,128)(2,1)S(1)}, bf16[2,256,256]{2,0,1:T(2,128)(2,1)S(1)}, u32[]{:S(2)}, u32[]{:S(2)}) collective-permute-start(bf16[2,256,256]{2,0,1:T(2,128)(2,1)S(1)} %slice.102), channel_id=1, source_target_pairs={{1,0},{2,1},{3,2},{4,3},{5,4},{6,5},{7,6},{8,7},{9,8},{10,9},{11,1... | collective-permute-start | bytes 786440 | tf_op jit(solution)/shard_map/ppermute | solution.py:18
Sparse Core Ops, SparseCore 0:
  59.6 84.0 all-reduce.1
where the time goes:
time: 152 us
  waiting for transfers between devices  86.4 us (57%)
  local copies, waits for them, and re-layouts  24.9 us (16%)
  other arithmetic  17.7 us (12%)
  between operations  13.6 us (9%)
  starting transfers between devices  8.56 us (6%)
    psum x1, waiting for transfers between devices, shards(): lax.psum(jnp.sum(picked.astype(jnp.float32) * weights[:, None, None], axi...  84.2 us
    select_n x7, other arithmetic, shift_rows(): jnp.where(taken[..., None], current[..., step_size:step_size + new_len],...  10.1 us
    ppermute x2, starting transfers between devices, passed_along(): lax.ppermute(value, axis, [(source, source + steps) for source in range(i...  8.56 us
    while x18, local copies, waits for them, and re-layouts  6.53 us
    reshape x2, local copies, waits for them, and re-layouts, toeplitz(): return flat.reshape(components, span, length + 1)[:, :, :width]  5.62 us
  transfers between devices with their start and end apart: 3, of which 2 were waited for; matrix products, arithmetic and copies ran while one was open for 3% of the time, Pallas kernels for 0%

commit v1 on v0

v1 whole, which is shorter than its diff:
```python
import math

import jax
import jax.numpy as jnp
from jax import lax
from jax.experimental import pallas as pl
from jax.experimental.pallas import tpu as pltpu
from jax.sharding import PartitionSpec as P

TLEN = 256
MAXM = 256
LANES = 128
PACK = 16


epsilon = 1e-05


def column_of(row, size):
    here = lax.broadcasted_iota(jnp.int32, (size, size), 0)
    there = lax.broadcasted_iota(jnp.int32, (size, size), 1)
    return jnp.sum(jnp.where(here == there, row, jnp.zeros_like(row)), axis=1, keepdims=True)


def stack_kernel(live_ref, own_ref, next_ref, template_ref, moveout_ref, order_ref, out_ref, frames_ref):
    components, stations, block = own_ref.shape
    kcount, taps = template_ref.shape[1:]
    columns = block + MAXM
    span = 2 * block
    lane = lax.broadcasted_iota(jnp.int32, (kcount, LANES), 1)
    total = jnp.zeros((kcount, block), jnp.float32)
    for s in range(stations):
        squares = jnp.zeros((1, span), jnp.float32)
        for c in range(components):
            signal = jnp.concatenate([own_ref[c, s : s + 1, :], next_ref[c, s : s + 1, :]], axis=1).astype(jnp.float32)
            squares = squares + signal * signal
            base = jnp.concatenate(
                [pltpu.roll(signal, span - r, 1) if r else signal for r in range(PACK)], axis=0
            )
            for q in range(LANES // PACK):
                moved = pltpu.roll(base, span - q * PACK, 1) if q else base
                moved = moved[:, : columns + LANES].astype(jnp.bfloat16)
                for h in range(TLEN // LANES):
                    start = c * TLEN + h * LANES + q * PACK
                    frames_ref[start : start + PACK, :] = moved[:, h * LANES : h * LANES + columns]
        energy = squares
        step = 1
        while step < TLEN:
            energy = energy + pltpu.roll(energy, span - step, 1)
            step *= 2
        record_scale = 1.0 / (taps * jnp.sqrt(energy[:, :columns] / taps + epsilon))
        weights = template_ref[s]
        wide = weights.astype(jnp.float32)
        template_scale = 1.0 / jnp.sqrt(jnp.sum(wide * wide, axis=1, keepdims=True) / taps + epsilon)
        correlation = jnp.dot(weights, frames_ref[...], preferred_element_type=jnp.float32)
        scores = (correlation * record_scale * template_scale).astype(jnp.bfloat16).astype(jnp.float32)
        moveout = column_of(moveout_ref[s : s + 1, :], kcount)
        low = moveout % LANES
        place = lane + low
        inside = place < LANES
        place = place % LANES
        far = moveout >= LANES
        turned = [
            jnp.take_along_axis(scores[:, i * LANES : (i + 1) * LANES], place, axis=1)
            for i in range(columns // LANES)
        ]
        near = [jnp.where(inside, turned[i], turned[i + 1]) for i in range(columns // LANES - 1)]
        picked = jnp.concatenate([jnp.where(far, near[i + 1], near[i]) for i in range(block // LANES)], axis=1)
        total = total + picked * live_ref[s].astype(jnp.float32)
    order = column_of(order_ref[...], kcount)
    chosen = order == lax.broadcasted_iota(jnp.int32, (kcount, kcount), 1)
    rows = jnp.dot(
        chosen.astype(jnp.bfloat16), total.astype(jnp.bfloat16), preferred_element_type=jnp.float32
    )
    out_ref[...] = rows.astype(jnp.bfloat16).reshape(out_ref.shape)


def shards(record, templates, moveouts, live_mask, owner_order):
    stations, components, block = record.shape
    kcount, taps = templates.shape[1:]
    count = lax.axis_size("tm")
    groups = lax.axis_size("sta")
    own = jnp.transpose(record, (1, 0, 2))
    ahead = lax.ppermute(own, "tm", [(source, source - 1) for source in range(1, count)])
    vmem = pl.BlockSpec(memory_space=pltpu.VMEM)
    partial = pl.pallas_call(
        stack_kernel,
        out_shape=jax.ShapeDtypeStruct((groups, kcount // groups, block), jnp.bfloat16),
        in_specs=[pl.BlockSpec(memory_space=pltpu.SMEM), vmem, vmem, vmem, vmem, vmem],
        out_specs=vmem,
        scratch_shapes=[pltpu.VMEM((taps, block + MAXM), jnp.bfloat16)],
        compiler_params=pltpu.CompilerParams(vmem_limit_bytes=40 << 20),
        name="stack",
    )(live_mask, own, ahead, templates, moveouts, owner_order.reshape(1, kcount))
    parts = lax.all_to_all(partial, "sta", 0, 0)
    stack_scale = math.sqrt(components * TLEN / (stations * groups))
    return jnp.sum(parts.astype(jnp.float32), axis=0) * stack_scale


def solution(mesh):
    placed = (P("sta", None, "tm"), P("sta", None, None), P("sta", None), P("sta"), P())
    return jax.shard_map(
        shards, mesh=mesh, in_specs=placed, out_specs=P("sta", "tm"), check_vma=False
    )
```

time: 152 us -> 26.2 us (0.17)
  the two profiles are of different devices: /device:TPU:32 before, /device:TPU:113 now
where the time goes in v1:
time: 26.2 us; the launch traced here: 26 us
  blocking collectives  10.3 us (39%)
  waiting for transfers between devices  6.18 us (24%)
  Pallas kernels  4.21 us (16%)
  starting transfers between devices  2.71 us (10%)
  local copies, waits for them, and re-layouts  1.83 us (7%)
  other arithmetic  0.67 us (3%)
    all_to_all x1, blocking collectives, shards(): parts = lax.all_to_all(partial, 'sta', 0, 0)  10.3 us
    ppermute x1, waiting for transfers between devices, shards(): lax.ppermute(own, 'tm', [(source, source - 1) for source in range(1, coun...  6.18 us
    pallas_call x1, Pallas kernels, shards(): pl.pallas_call(stack_kernel, out_shape=jax.ShapeDtypeStruct((groups, kcou...  4.21 us
    ppermute x1, starting transfers between devices, shards(): lax.ppermute(own, 'tm', [(source, source - 1) for source in range(1, coun...  2.71 us
    unnamed x10, local copies, waits for them, and re-layouts  1.83 us
    mul x1, other arithmetic, shards(): return jnp.sum(parts.astype(jnp.float32), axis=0) * stack_scale  0.64 us
  transfers between devices with their start and end apart: 1, of which 1 were waited for; matrix products, arithmetic and copies ran while one was open for 0% of the time, Pallas kernels for 0%

profile of v1, /device:TPU:113, one launch (start us, length us, event | category | flops | bytes accessed | tf_op | source)
XLA Modules:
  0.0 26.0 jit_solution(919083706669376115)
XLA Ops:
  0.0 0.0 copy-start.2
  0.0 0.0 copy-start.3
  0.0 0.0 copy-start.4
  0.0 2.7 %collective-permute-start = (bf16[3,2,512]{2,1,0:T(2,128)(2,1)}, bf16[3,2,512]{2,1,0:T(2,128)(2,1)S(1)}, u32[]{:S(2)}, u32[]{:S(2)}) collective-permute-start(bf16[3,2,512]{2,1,0:T(2,128)(2,1)} %bitcast.2), channel_id=1, source_target_pairs={{1,0},{2,1},{3,2},{4,3},{5,4},{6,5},{7,6},{8,7},{9,8},{10,9},{11,1... | collective-permute-start | bytes 18440 | tf_op jit(solution)/shard_map/ppermute | solution.py:84
  2.7 6.2 %collective-permute-done.next_ref = bf16[3,2,512]{2,1,0:T(2,128)(2,1)S(1)} collective-permute-done((bf16[3,2,512]{2,1,0:T(2,128)(2,1)}, bf16[3,2,512]{2,1,0:T(2,128)(2,1)S(1)}, u32[]{:S(2)}, u32[]{:S(2)}) %collective-permute-start) | collective-permute-done | bytes 6176 | tf_op jit(solution)/shard_map/ppermute | solution.py:84
  8.9 0.0 copy-done.2
  8.9 0.0 copy-done.3
  8.9 0.0 copy-done.4
  8.9 0.0 copy-start
  8.9 1.1 %copy-done = bf16[2,256,768]{2,1,0:T(8,128)(2,1)S(1)} copy-done((bf16[2,256,768]{2,1,0:T(8,128)(2,1)S(1)}, bf16[2,256,768]{2,1,0:T(8,128)(2,1)}, u32[]{:S(2)}) %copy-start) | copy-done | bytes 786456
  10.1 0.0 copy-start.1
  10.1 0.7 %copy-done.1 = bf16[2,3,512]{2,0,1:T(2,128)(2,1)S(1)} copy-done((bf16[2,3,512]{2,0,1:T(2,128)(2,1)S(1)}, bf16[2,3,512]{2,0,1:T(2,128)(2,1)}, u32[]{:S(2)}) %copy-start.1) | copy-done | bytes 6168
  10.8 4.2 %stack.1 = bf16[8,32,512]{2,1,0:T(8,128)(2,1)S(1)} custom-call(s32[2]{0:T(128)S(1)} %copy-done.4, bf16[3,2,512]{2,1,0:T(2,128)(2,1)S(1)} %bitcast.3, bf16[3,2,512]{2,1,0:T(2,128)(2,1)S(1)} %collective-permute-done.next_ref, bf16[2,256,768]{2,1,0:T(8,128)(2,1)S(1)} %copy-done, s32[2,256]{1,0:T(2,128)S(1)} %copy-done.2, s32[1,256]{1,0:T(1,128)S(1)} %bitcast.4), custom_call_target="tpu_custom_call" | custom-call | tf_op jit(solution)/shard_map/stack/pallas_call | solution.py:86
  15.0 10.3 %all_to_all.5 = bf16[8,32,512]{2,1,0:T(8,128)(2,1)S(1)} all-to-all(bf16[8,32,512]{2,1,0:T(8,128)(2,1)S(1)} %stack.1), channel_id=1, replica_groups=mesh['sta'=8,'tm'=32] {'sta'}, dimensions={0} | all-to-all | bytes 524288 | tf_op jit(solution)/shard_map/all_to_all | solution.py:95
  25.3 0.6 %broadcast_multiply_fusion = f32[32,512]{1,0:T(8,128)} fusion(f32[32,512]{1,0:T(8,128)S(1)} %convert_reduce_fusion), kind=kLoop, calls=%fused_computation.1 | loop fusion | flops 16384 | bytes 131072 | tf_op jit(solution)/shard_map/mul | solution.py:97
  (1 shorter events, 0.0 us)
Async XLA Ops:
  0.0 8.9 %copy-start.2 = (s32[2,256]{1,0:T(2,128)S(1)}, s32[2,256]{1,0:T(2,128)}, u32[]{:S(2)}) copy-start(s32[2,256]{1,0:T(2,128)} %moveout_ref.1) | copy-start | bytes 6148
  0.0 8.9 %copy-start.3 = (s32[256]{0:T(256)S(1)}, s32[256]{0:T(256)}, u32[]{:S(2)}) copy-start(s32[256]{0:T(256)} %param.9) | copy-start | bytes 3076
  0.0 8.9 %copy-start.4 = (s32[2]{0:T(128)S(1)}, s32[2]{0:T(128)}, u32[]{:S(2)}) copy-start(s32[2]{0:T(128)} %live_ref.1) | copy-start | bytes 28
  0.0 8.9 %collective-permute-start = (bf16[3,2,512]{2,1,0:T(2,128)(2,1)}, bf16[3,2,512]{2,1,0:T(2,128)(2,1)S(1)}, u32[]{:S(2)}, u32[]{:S(2)}) collective-permute-start(bf16[3,2,512]{2,1,0:T(2,128)(2,1)} %bitcast.2), channel_id=1, source_target_pairs={{1,0},{2,1},{3,2},{4,3},{5,4},{6,5},{7,6},{8,7},{9,8},{10,9},{11,1... | collective-permute-start | bytes 18440 | tf_op jit(solution)/shard_map/ppermute | solution.py:84
  8.9 1.1 %copy-start = (bf16[2,256,768]{2,1,0:T(8,128)(2,1)S(1)}, bf16[2,256,768]{2,1,0:T(8,128)(2,1)}, u32[]{:S(2)}) copy-start(bf16[2,256,768]{2,1,0:T(8,128)(2,1)} %template_ref.1) | copy-start | bytes 2359300
  10.1 0.7 %copy-start.1 = (bf16[2,3,512]{2,0,1:T(2,128)(2,1)S(1)}, bf16[2,3,512]{2,0,1:T(2,128)(2,1)}, u32[]{:S(2)}) copy-start(bf16[2,3,512]{2,0,1:T(2,128)(2,1)} %param.5) | copy-start | bytes 18436

commit v2 on v1

v2 whole, which is shorter than its diff:
```python
import math

import jax
import jax.numpy as jnp
from jax import lax
from jax.experimental import pallas as pl
from jax.experimental.pallas import tpu as pltpu
from jax.sharding import PartitionSpec as P
TLEN = 256
MAXM = 256
LANES = 128
SPAN = 16
epsilon = 1e-05


def column_of(row, size):
    here = lax.broadcasted_iota(jnp.int32, (size, size), 0)
    there = lax.broadcasted_iota(jnp.int32, (size, size), 1)
    return jnp.sum(jnp.where(here == there, row, jnp.zeros_like(row)), axis=1, keepdims=True)


def block_of(array, i):
    return array[:, i * LANES : (i + 1) * LANES]


def backwards(ref, blocks):
    components, stations = ref.shape[:2]
    rows = jnp.concatenate([ref[c].astype(jnp.float32) for c in range(components)], axis=0)
    rows = jnp.concatenate([rows, jnp.zeros((-rows.shape[0] % 8, rows.shape[1]), jnp.float32)], axis=0)
    mirror = LANES - 1 - lax.broadcasted_iota(jnp.int32, (rows.shape[0], LANES), 1)
    return [jnp.take_along_axis(block_of(rows, i), mirror, axis=1) for i in reversed(blocks)]


def staircase(row, count, step):
    return pltpu.roll(jnp.broadcast_to(row, (count, row.shape[1])), 0, 1, stride=step, stride_axis=0)


def record_scale_of(rows, stations, s, taps):
    squares = sum(jnp.square(rows[r : r + 1]) for r in range(s, taps // TLEN * stations, stations))
    energy = jnp.sum(staircase(squares, SPAN, 1), axis=0, keepdims=True)
    energy = jnp.sum(staircase(energy, LANES // SPAN, SPAN), axis=0, keepdims=True)
    energy = energy + pltpu.roll(energy, LANES, 1)
    return 1.0 / (taps * jnp.sqrt(energy / taps + epsilon))


def lag(moveout):
    return lax.broadcasted_iota(jnp.int32, moveout.shape, 1) + (moveout & (LANES - 1))


def turn(correlation, record_scale, template_scale, reach):
    score = (correlation * record_scale * template_scale).astype(jnp.bfloat16).astype(jnp.float32)
    return jnp.take_along_axis(score, LANES - 1 - (reach & (LANES - 1)), axis=1)


def near_kernel(
    live_ref, own_ref, template_ref, moveout_ref, order_ref,
    factor_ref, scale_ref, delay_ref, chosen_ref, corner_ref, joined_ref, turned_ref, frames_ref, *, gain
):
    components, stations, block = own_ref.shape
    kcount, taps = template_ref.shape[1:]
    rows = jnp.concatenate(backwards(own_ref, range(block // LANES)), axis=1)
    last = block // LANES - 1
    for s in range(stations):
        for c in range(components):
            r = c * stations + s
            steps = staircase(rows[r : r + 1], LANES, 1).astype(jnp.bfloat16)
            corner_ref[s, c * LANES : (c + 1) * LANES, :] = block_of(steps, last - 2)
            for h in range(TLEN // LANES):
                start = c * TLEN + h * LANES
                frames_ref[s, start : start + LANES, :] = steps[:, (last - 1 - h) * LANES : (last + 1 - h) * LANES]
        record_scale = record_scale_of(rows, stations, s, taps)
        wide = template_ref[s].astype(jnp.float32)
        energy = jnp.sum(wide * wide, axis=1, keepdims=True)
        scale = jnp.broadcast_to(1.0 / jnp.sqrt(energy / taps + epsilon), (kcount, LANES))
        scale_ref[s] = scale
        moveout = jnp.broadcast_to(column_of(moveout_ref[s : s + 1, :], kcount), (kcount, LANES))
        delay_ref[s] = moveout
        correlation = jnp.dot(template_ref[s], frames_ref[s], preferred_element_type=jnp.float32)
        reach = lag(moveout)
        first = turn(block_of(correlation, 1), block_of(record_scale, last), scale, reach)
        second = turn(block_of(correlation, 0), block_of(record_scale, last - 1), scale, reach)
        joined_ref[s] = jnp.where(reach < LANES, first, second)
        turned_ref[s] = second
        factor_ref[s] = jnp.broadcast_to(live_ref[0:1, s : s + 1].astype(jnp.float32) * gain, (8, LANES))
    order = column_of(order_ref[...], kcount)
    chosen_ref[...] = (order == lax.broadcasted_iota(jnp.int32, (kcount, kcount), 1)).astype(jnp.bfloat16)


def stack_kernel(
    own_ref, next_ref, template_ref, factor_ref, scale_ref, delay_ref, chosen_ref, corner_ref, joined_ref, turned_ref,
    out_ref, frames_ref
):
    components, stations, block = own_ref.shape
    kcount, taps = template_ref.shape[1:]
    count = block // LANES
    rows = jnp.concatenate(
        backwards(next_ref, range(count)) + backwards(own_ref, range(count - 2, count)), axis=1
    )
    total = [jnp.zeros((kcount, LANES), jnp.float32) for _ in range(count)]
    for s in range(stations):
        for c in range(components):
            r = c * stations + s
            steps = staircase(rows[r : r + 1, : (count + 1) * LANES], LANES, 1).astype(jnp.bfloat16)
            start = c * TLEN
            frames_ref[s, start : start + LANES, : (count - 1) * LANES] = steps[:, 2 * LANES :]
            frames_ref[s, start : start + LANES, (count - 1) * LANES :] = corner_ref[s, c * LANES : (c + 1) * LANES, :]
            frames_ref[s, start + LANES : start + TLEN, :] = steps[:, LANES:]
    for s in range(stations):
        record_scale = record_scale_of(rows, stations, s, taps)
        correlation = jnp.dot(template_ref[s], frames_ref[s], preferred_element_type=jnp.float32)
        moveout = delay_ref[s]
        reach = lag(moveout)
        far = moveout >= LANES
        factor = factor_ref[s, 0:1]
        turned = [turned_ref[s]] + [
            turn(block_of(correlation, i), block_of(record_scale, 2 + i), scale_ref[s], reach)
            for i in reversed(range(count))
        ]
        joined = [joined_ref[s]] + [jnp.where(reach < LANES, turned[i], turned[i + 1]) for i in range(count)]
        for i in range(count):
            total[i] = total[i] + jnp.where(far, joined[i + 1], joined[i]) * factor
    stacked = jnp.concatenate(total, axis=1).astype(jnp.bfloat16)
    placed = jnp.dot(chosen_ref[...], stacked, preferred_element_type=jnp.float32)
    out_ref[...] = placed.astype(jnp.bfloat16).reshape(out_ref.shape)


def near_part(own, templates, moveouts, live_mask, owner_order, gain):
    components, stations, block = own.shape
    kcount, taps = templates.shape[1:]
    vmem = pl.BlockSpec(memory_space=pltpu.VMEM)
    row = (stations, kcount, LANES)
    shapes = [
        ((stations, 8, LANES), jnp.float32), (row, jnp.float32), (row, jnp.int32), ((kcount, kcount), jnp.bfloat16),
        ((stations, taps // 2, LANES), jnp.bfloat16), (row, jnp.float32), (row, jnp.float32),
    ]
    return pl.pallas_call(
        lambda *refs: near_kernel(*refs, gain=gain),
        out_shape=[jax.ShapeDtypeStruct(*shape) for shape in shapes],
        in_specs=[vmem] * 5,
        out_specs=[vmem] * len(shapes),
        scratch_shapes=[pltpu.VMEM((stations, taps, 2 * LANES), jnp.bfloat16)],
        compiler_params=pltpu.CompilerParams(vmem_limit_bytes=32 << 20),
        name="near",
    )(live_mask.reshape(1, stations), own, templates, moveouts, owner_order.reshape(1, kcount))


def stack_part(own, ahead, templates, near, groups):
    components, stations, block = own.shape
    kcount, taps = templates.shape[1:]
    vmem = pl.BlockSpec(memory_space=pltpu.VMEM)
    return pl.pallas_call(
        stack_kernel,
        out_shape=jax.ShapeDtypeStruct((groups, kcount // groups, block), jnp.bfloat16),
        in_specs=[vmem] * (3 + len(near)),
        out_specs=vmem,
        scratch_shapes=[pltpu.VMEM((stations, taps, block), jnp.bfloat16)],
        compiler_params=pltpu.CompilerParams(vmem_limit_bytes=32 << 20),
        name="stack",
    )(own, ahead, templates, *near)


def shards(record, templates, moveouts, live_mask, owner_order):
    stations, components = record.shape[:2]
    count = lax.axis_size("tm")
    groups = lax.axis_size("sta")
    own = jnp.transpose(record, (1, 0, 2))
    ahead = lax.ppermute(own, "tm", [(source, source - 1) for source in range(1, count)])
    gain = math.sqrt(components * TLEN / (stations * groups))
    near = near_part(own, templates, moveouts, live_mask, owner_order, gain)
    partial = stack_part(own, ahead, templates, near, groups)
    parts = lax.all_to_all(partial, "sta", 0, 0)
    return jnp.sum(parts.astype(jnp.float32), axis=0)


def solution(mesh):
    placed = (P("sta", None, "tm"), P("sta", None, None), P("sta", None), P("sta"), P())
    return jax.shard_map(
        shards, mesh=mesh, in_specs=placed, out_specs=P("sta", "tm"), check_vma=False
    )
```

time: 26.2 us -> 22.3 us (0.85)
  the two profiles are of different devices: /device:TPU:113 before, /device:TPU:192 now
where the time goes in v2:
time: 22.3 us; the launch traced here: 22.1 us
  blocking collectives  11.1 us (50%)
  starting transfers between devices  5.1 us (23%)
  Pallas kernels  2.59 us (12%)
  local copies, waits for them, and re-layouts  2.49 us (11%)
  other arithmetic  0.67 us (3%)
    all_to_all x1, blocking collectives, shards(): parts = lax.all_to_all(partial, 'sta', 0, 0)  11.1 us
    ppermute x1, starting transfers between devices, shards(): lax.ppermute(own, 'tm', [(source, source - 1) for source in range(1, coun...  5.1 us
    unnamed x12, local copies, waits for them, and re-layouts  2.49 us
    pallas_call x1, Pallas kernels, near_part(): pl.pallas_call(lambda *refs: near_kernel(*refs, gain=gain), out_shape=[ja...  1.34 us
    pallas_call x1, Pallas kernels, stack_part(): pl.pallas_call(stack_kernel, out_shape=jax.ShapeDtypeStruct((groups, kcou...  1.25 us
    reduce_sum x1, other arithmetic, shards(): return jnp.sum(parts.astype(jnp.float32), axis=0)  0.67 us
  transfers between devices with their start and end apart: 1, of which 0 were waited for; matrix products, arithmetic and copies ran while one was open for 0% of the time, Pallas kernels for 6%

profile of v2, /device:TPU:192, one launch (start us, length us, event | category | flops | bytes accessed | tf_op | source)
XLA Modules:
  0.0 22.1 jit_solution(10151958924904574925)
XLA Ops:
  0.0 0.0 copy-start.3
  0.0 5.1 %collective-permute-start = (bf16[3,2,512]{2,1,0:T(2,128)(2,1)}, bf16[3,2,512]{2,1,0:T(2,128)(2,1)S(1)}, u32[]{:S(2)}, u32[]{:S(2)}) collective-permute-start(bf16[3,2,512]{2,1,0:T(2,128)(2,1)} %bitcast.3), channel_id=1, source_target_pairs={{1,0},{2,1},{3,2},{4,3},{5,4},{6,5},{7,6},{8,7},{9,8},{10,9},{11,1... | collective-permute-start | bytes 18440 | tf_op jit(solution)/shard_map/ppermute | solution.py:167
  5.1 0.0 copy-start.4
  5.1 0.0 copy-start.5
  5.1 0.0 copy-done.3
  5.1 0.7 %copy-done.4 = s32[256]{0:T(256)S(1)} copy-done((s32[256]{0:T(256)S(1)}, s32[256]{0:T(256)}, u32[]{:S(2)}) %copy-start.4) | copy-done | bytes 1048
  5.8 0.0 copy-done.5
  5.8 0.0 copy-start
  5.8 1.1 %copy-done = bf16[2,256,768]{2,1,0:T(8,128)(2,1)S(1)} copy-done((bf16[2,256,768]{2,1,0:T(8,128)(2,1)S(1)}, bf16[2,256,768]{2,1,0:T(8,128)(2,1)}, u32[]{:S(2)}) %copy-start) | copy-done | bytes 786456
  6.9 0.0 copy-start.2
  6.9 0.7 %copy-done.2 = bf16[2,3,512]{2,0,1:T(2,128)(2,1)S(1)} copy-done((bf16[2,3,512]{2,0,1:T(2,128)(2,1)S(1)}, bf16[2,3,512]{2,0,1:T(2,128)(2,1)}, u32[]{:S(2)}) %copy-start.2) | copy-done | bytes 6168
  7.6 0.0 copy-start.1
  7.6 1.3 %near.1 = (f32[2,8,128]{2,1,0:T(8,128)S(1)}, f32[2,256,128]{2,1,0:T(8,128)S(1)}, s32[2,256,128]{2,1,0:T(8,128)S(1)}, bf16[256,256]{1,0:T(8,128)(2,1)S(1)}, bf16[...) custom-call(s32[1,2]{1,0:T(1,128)S(1)} %bitcast.7, ...), custom_call_target="tpu_custom_call" | custom-call | tf_op jit(solution)/shard_map/near/pallas_call | solution.py:136
  9.0 0.0 collective-permute-done.next_ref
  9.0 0.0 copy-done.1
  9.0 1.2 %stack.1 = bf16[8,32,512]{2,1,0:T(8,128)(2,1)S(1)} custom-call(bf16[3,2,512]{2,1,0:T(2,128)(2,1)S(1)} %bitcast.5, bf16[3,2,512]{2,1,0:T(2,128)(2,1)S(1)} %collective-permute-done.next_ref, bf16[2,256,768]{2,1,0:T(8,128)(2,1)S(1)} %copy-done.1, f32[2,8,128]{2,1,0:T(8,128)S(1)} %get-tuple-element.12.factor_ref, ...), custom_call_target="tpu_custom_call" | custom-call | tf_op jit(solution)/shard_map/stack/pallas_call | solution.py:151
  10.2 11.1 %all_to_all.5 = bf16[8,32,512]{2,1,0:T(8,128)(2,1)S(1)} all-to-all(bf16[8,32,512]{2,1,0:T(8,128)(2,1)S(1)} %stack.1), channel_id=1, replica_groups=mesh['sta'=8,'tm'=32] {'sta'}, dimensions={0} | all-to-all | bytes 524288 | tf_op jit(solution)/shard_map/all_to_all | solution.py:171
  21.4 0.7 %convert_reduce_fusion = f32[32,512]{1,0:T(8,128)} fusion(bf16[8,32,512]{2,1,0:T(8,128)(2,1)S(1)} %all_to_all.5), kind=kLoop, calls=%fused_computation | loop fusion | flops 245760 | bytes 327680 | tf_op jit(solution)/shard_map/reduce_sum | solution.py:172
Async XLA Ops:
  0.0 5.1 %copy-start.3 = (s32[2,256]{1,0:T(2,128)S(1)}, s32[2,256]{1,0:T(2,128)}, u32[]{:S(2)}) copy-start(s32[2,256]{1,0:T(2,128)} %refs_3_.1) | copy-start | bytes 6148
  0.0 9.0 %collective-permute-start = (bf16[3,2,512]{2,1,0:T(2,128)(2,1)}, bf16[3,2,512]{2,1,0:T(2,128)(2,1)S(1)}, u32[]{:S(2)}, u32[]{:S(2)}) collective-permute-start(bf16[3,2,512]{2,1,0:T(2,128)(2,1)} %bitcast.3), channel_id=1, source_target_pairs={{1,0},{2,1},{3,2},{4,3},{5,4},{6,5},{7,6},{8,7},{9,8},{10,9},{11,1... | collective-permute-start | bytes 18440 | tf_op jit(solution)/shard_map/ppermute | solution.py:167
  5.1 0.7 %copy-start.4 = (s32[256]{0:T(256)S(1)}, s32[256]{0:T(256)}, u32[]{:S(2)}) copy-start(s32[256]{0:T(256)} %param.9) | copy-start | bytes 3076
  5.1 0.7 %copy-start.5 = (s32[2]{0:T(128)S(1)}, s32[2]{0:T(128)}, u32[]{:S(2)}) copy-start(s32[2]{0:T(128)} %param.8) | copy-start | bytes 28
  5.8 1.1 %copy-start = (bf16[2,256,768]{2,1,0:T(8,128)(2,1)S(1)}, bf16[2,256,768]{2,1,0:T(8,128)(2,1)}, u32[]{:S(2)}) copy-start(bf16[2,256,768]{2,1,0:T(8,128)(2,1)} %template_ref.1) | copy-start | bytes 2359300
  6.9 0.7 %copy-start.2 = (bf16[2,3,512]{2,0,1:T(2,128)(2,1)S(1)}, bf16[2,3,512]{2,0,1:T(2,128)(2,1)}, u32[]{:S(2)}) copy-start(bf16[2,3,512]{2,0,1:T(2,128)(2,1)} %param.5) | copy-start | bytes 18436
  7.6 1.4 %copy-start.1 = (bf16[2,256,768]{2,1,0:T(8,128)(2,1)S(1)}, bf16[2,256,768]{2,1,0:T(8,128)(2,1)}, u32[]{:S(2)}) copy-start(bf16[2,256,768]{2,1,0:T(8,128)(2,1)} %template_ref.1) | copy-start | bytes 2359300

commit v3 on v2

--- a/solution.py
+++ b/solution.py
@@ -53,13 +53,25 @@
 
 
 def near_kernel(
-    live_ref, own_ref, template_ref, moveout_ref, order_ref,
-    factor_ref, scale_ref, delay_ref, chosen_ref, corner_ref, joined_ref, turned_ref, frames_ref, *, gain
+    live_hbm, own_hbm, template_hbm, moveout_hbm, order_hbm,
+    template_ref, tail_ref, factor_ref, scale_ref, delay_ref, chosen_ref, corner_ref, joined_ref, turned_ref,
+    live_ref, own_ref, moveout_ref, order_ref, frames_ref, small_sem, template_sem, *, gain
 ):
     components, stations, block = own_ref.shape
     kcount, taps = template_ref.shape[1:]
-    rows = jnp.concatenate(backwards(own_ref, range(block // LANES)), axis=1)
+    pairs = [(own_hbm, own_ref), (moveout_hbm, moveout_ref), (order_hbm, order_ref), (live_hbm, live_ref)]
+    small = [pltpu.make_async_copy(*pair, small_sem.at[i]) for i, pair in enumerate(pairs)]
+    large = [
+        pltpu.make_async_copy(template_hbm.at[s], template_ref.at[s], template_sem.at[s]) for s in range(stations)
+    ]
+    for copy in small + large:
+        copy.start()
+    small[0].wait()
+    blocks = backwards(own_ref, range(block // LANES))
+    rows = jnp.concatenate(blocks, axis=1)
     last = block // LANES - 1
+    for i in range(2):
+        tail_ref[:, i * LANES : (i + 1) * LANES] = blocks[i]
     for s in range(stations):
         for c in range(components):
             r = c * stations + s
@@ -68,34 +80,36 @@
             for h in range(TLEN // LANES):
                 start = c * TLEN + h * LANES
                 frames_ref[s, start : start + LANES, :] = steps[:, (last - 1 - h) * LANES : (last + 1 - h) * LANES]
+    for copy in small[1:]:
+        copy.wait()
+    order = column_of(order_ref[...], kcount)
+    chosen_ref[...] = (order == lax.broadcasted_iota(jnp.int32, (kcount, kcount), 1)).astype(jnp.bfloat16)
+    for s in range(stations):
+        delay_ref[s] = jnp.broadcast_to(column_of(moveout_ref[s : s + 1, :], kcount), (kcount, LANES))
+        factor_ref[s] = jnp.broadcast_to(live_ref[0:1, s : s + 1].astype(jnp.float32) * gain, (8, LANES))
+    for s in range(stations):
+        large[s].wait()
         record_scale = record_scale_of(rows, stations, s, taps)
         wide = template_ref[s].astype(jnp.float32)
         energy = jnp.sum(wide * wide, axis=1, keepdims=True)
         scale = jnp.broadcast_to(1.0 / jnp.sqrt(energy / taps + epsilon), (kcount, LANES))
         scale_ref[s] = scale
-        moveout = jnp.broadcast_to(column_of(moveout_ref[s : s + 1, :], kcount), (kcount, LANES))
-        delay_ref[s] = moveout
         correlation = jnp.dot(template_ref[s], frames_ref[s], preferred_element_type=jnp.float32)
-        reach = lag(moveout)
+        reach = lag(delay_ref[s])
         first = turn(block_of(correlation, 1), block_of(record_scale, last), scale, reach)
         second = turn(block_of(correlation, 0), block_of(record_scale, last - 1), scale, reach)
         joined_ref[s] = jnp.where(reach < LANES, first, second)
         turned_ref[s] = second
-        factor_ref[s] = jnp.broadcast_to(live_ref[0:1, s : s + 1].astype(jnp.float32) * gain, (8, LANES))
-    order = column_of(order_ref[...], kcount)
-    chosen_ref[...] = (order == lax.broadcasted_iota(jnp.int32, (kcount, kcount), 1)).astype(jnp.bfloat16)
 
 
 def stack_kernel(
-    own_ref, next_ref, template_ref, factor_ref, scale_ref, delay_ref, chosen_ref, corner_ref, joined_ref, turned_ref,
+    next_ref, template_ref, tail_ref, factor_ref, scale_ref, delay_ref, chosen_ref, corner_ref, joined_ref, turned_ref,
     out_ref, frames_ref
 ):
-    components, stations, block = own_ref.shape
+    components, stations, block = next_ref.shape
     kcount, taps = template_ref.shape[1:]
     count = block // LANES
-    rows = jnp.concatenate(
-        backwards(next_ref, range(count)) + backwards(own_ref, range(count - 2, count)), axis=1
-    )
+    rows = jnp.concatenate(backwards(next_ref, range(count)) + [tail_ref[...]], axis=1)
     total = [jnp.zeros((kcount, LANES), jnp.float32) for _ in range(count)]
     for s in range(stations):
         for c in range(components):
@@ -127,36 +141,47 @@
 def near_part(own, templates, moveouts, live_mask, owner_order, gain):
     components, stations, block = own.shape
     kcount, taps = templates.shape[1:]
-    vmem = pl.BlockSpec(memory_space=pltpu.VMEM)
     row = (stations, kcount, LANES)
     shapes = [
+        (templates.shape, jnp.bfloat16), ((-(-components * stations // 8) * 8, 2 * LANES), jnp.float32),
         ((stations, 8, LANES), jnp.float32), (row, jnp.float32), (row, jnp.int32), ((kcount, kcount), jnp.bfloat16),
         ((stations, taps // 2, LANES), jnp.bfloat16), (row, jnp.float32), (row, jnp.float32),
     ]
     return pl.pallas_call(
         lambda *refs: near_kernel(*refs, gain=gain),
         out_shape=[jax.ShapeDtypeStruct(*shape) for shape in shapes],
-        in_specs=[vmem] * 5,
-        out_specs=[vmem] * len(shapes),
-        scratch_shapes=[pltpu.VMEM((stations, taps, 2 * LANES), jnp.bfloat16)],
+        in_specs=[pl.BlockSpec(memory_space=pltpu.HBM)] * 5,
+        out_specs=[pl.BlockSpec(memory_space=pltpu.VMEM)] * len(shapes),
+        scratch_shapes=[
+            pltpu.VMEM((1, stations), jnp.int32),
+            pltpu.VMEM(own.shape, own.dtype),
+            pltpu.VMEM(moveouts.shape, moveouts.dtype),
+            pltpu.VMEM((1, kcount), jnp.int32),
+            pltpu.VMEM((stations, taps, 2 * LANES), jnp.bfloat16),
+            pltpu.SemaphoreType.DMA((4,)),
+            pltpu.SemaphoreType.DMA((stations,)),
+        ],
         compiler_params=pltpu.CompilerParams(vmem_limit_bytes=32 << 20),
         name="near",
-    )(live_mask.reshape(1, stations), own, templates, moveouts, owner_order.reshape(1, kcount))
-
-
-def stack_part(own, ahead, templates, near, groups):
-    components, stations, block = own.shape
-    kcount, taps = templates.shape[1:]
+    )(*(
+        pltpu.with_memory_space_constraint(operand, pltpu.HBM)
+        for operand in (live_mask.reshape(1, stations), own, templates, moveouts, owner_order.reshape(1, kcount))
+    ))
+
+
+def stack_part(ahead, near, groups):
+    components, stations, block = ahead.shape
+    kcount, taps = near[0].shape[1:]
     vmem = pl.BlockSpec(memory_space=pltpu.VMEM)
     return pl.pallas_call(
         stack_kernel,
         out_shape=jax.ShapeDtypeStruct((groups, kcount // groups, block), jnp.bfloat16),
-        in_specs=[vmem] * (3 + len(near)),
+        in_specs=[vmem] * (1 + len(near)),
         out_specs=vmem,
         scratch_shapes=[pltpu.VMEM((stations, taps, block), jnp.bfloat16)],
         compiler_params=pltpu.CompilerParams(vmem_limit_bytes=32 << 20),
         name="stack",
-    )(own, ahead, templates, *near)
+    )(ahead, *near)
 
 
 def shards(record, templates, moveouts, live_mask, owner_order):
@@ -167,7 +192,7 @@
     ahead = lax.ppermute(own, "tm", [(source, source - 1) for source in range(1, count)])
     gain = math.sqrt(components * TLEN / (stations * groups))
     near = near_part(own, templates, moveouts, live_mask, owner_order, gain)
-    partial = stack_part(own, ahead, templates, near, groups)
+    partial = stack_part(ahead, near, groups)
     parts = lax.all_to_all(partial, "sta", 0, 0)
     return jnp.sum(parts.astype(jnp.float32), axis=0)
 

time: 22.3 us -> 21.2 us (0.951)
  the two profiles are of different devices: /device:TPU:192 before, /device:TPU:113 now
where the time goes in v3:
time: 21.2 us; the launch traced here: 21 us
  blocking collectives  10.3 us (49%)
  waiting for transfers between devices  3.82 us (18%)
  Pallas kernels  3.56 us (17%)
  starting transfers between devices  2.57 us (12%)
  other arithmetic  0.67 us (3%)
    all_to_all x1, blocking collectives, shards(): parts = lax.all_to_all(partial, 'sta', 0, 0)  10.3 us
    ppermute x1, waiting for transfers between devices, shards(): lax.ppermute(own, 'tm', [(source, source - 1) for source in range(1, coun...  3.82 us
    ppermute x1, starting transfers between devices, shards(): lax.ppermute(own, 'tm', [(source, source - 1) for source in range(1, coun...  2.57 us
    pallas_call x1, Pallas kernels, near_part(): pl.pallas_call(lambda *refs: near_kernel(*refs, gain=gain), out_shape=[ja...  2.35 us
    pallas_call x1, Pallas kernels, stack_part(): pl.pallas_call(stack_kernel, out_shape=jax.ShapeDtypeStruct((groups, kcou...  1.21 us
    reduce_sum x1, other arithmetic, shards(): return jnp.sum(parts.astype(jnp.float32), axis=0)  0.67 us
  transfers between devices with their start and end apart: 1, of which 1 were waited for; matrix products, arithmetic and copies ran while one was open for 0% of the time, Pallas kernels for 11%

profile of v3, /device:TPU:113, one launch (start us, length us, event | category | flops | bytes accessed | tf_op | source)
XLA Modules:
  0.0 21.0 jit_solution(16530029161541719693)
XLA Ops:
  0.0 2.6 %collective-permute-start = (bf16[3,2,512]{2,1,0:T(2,128)(2,1)}, bf16[3,2,512]{2,1,0:T(2,128)(2,1)S(1)}, u32[]{:S(2)}, u32[]{:S(2)}) collective-permute-start(bf16[3,2,512]{2,1,0:T(2,128)(2,1)} %bitcast.3), channel_id=1, source_target_pairs={{1,0},{2,1},{3,2},{4,3},{5,4},{6,5},{7,6},{8,7},{9,8},{10,9},{11,1... | collective-permute-start | bytes 18440 | tf_op jit(solution)/shard_map/ppermute | solution.py:192
  2.6 2.4 %near.1 = (bf16[2,256,768]{2,1,0:T(8,128)(2,1)S(1)}, f32[8,256]{1,0:T(8,128)S(1)}, f32[2,8,128]{2,1,0:T(8,128)S(1)}, f32[2,256,128]{2,1,0:T(8,128)S(1)}, s32[2,2...) custom-call(s32[1,2]{1,0:T(1,128)} %bitcast.6, ...), custom_call_target="tpu_custom_call" | custom-call | tf_op jit(solution)/shard_map/near/pallas_call | solution.py:150
  4.9 3.8 %collective-permute-done.next_ref = bf16[3,2,512]{2,1,0:T(2,128)(2,1)S(1)} collective-permute-done((bf16[3,2,512]{2,1,0:T(2,128)(2,1)}, bf16[3,2,512]{2,1,0:T(2,128)(2,1)S(1)}, u32[]{:S(2)}, u32[]{:S(2)}) %collective-permute-start) | collective-permute-done | bytes 6176 | tf_op jit(solution)/shard_map/ppermute | solution.py:192
  8.8 1.2 %stack.1 = bf16[8,32,512]{2,1,0:T(8,128)(2,1)S(1)} custom-call(bf16[3,2,512]{2,1,0:T(2,128)(2,1)S(1)} %collective-permute-done.next_ref, bf16[2,256,768]{2,1,0:T(8,128)(2,1)S(1)} %get-tuple-element.14.template_ref, f32[8,256]{1,0:T(8,128)S(1)} %get-tuple-element.15.tail_ref, f32[2,8,128]{2,1,0:T(8,128)S(1)} %get-tuple-element.16.factor_ref, ...), custom_call_target="tpu_custom_call" | custom-call | tf_op jit(solution)/shard_map/stack/pallas_call | solution.py:176
  10.0 10.3 %all_to_all.5 = bf16[8,32,512]{2,1,0:T(8,128)(2,1)S(1)} all-to-all(bf16[8,32,512]{2,1,0:T(8,128)(2,1)S(1)} %stack.1), channel_id=1, replica_groups=mesh['sta'=8,'tm'=32] {'sta'}, dimensions={0} | all-to-all | bytes 524288 | tf_op jit(solution)/shard_map/all_to_all | solution.py:196
  20.3 0.7 %convert_reduce_fusion = f32[32,512]{1,0:T(8,128)} fusion(bf16[8,32,512]{2,1,0:T(8,128)(2,1)S(1)} %all_to_all.5), kind=kLoop, calls=%fused_computation | loop fusion | flops 245760 | bytes 327680 | tf_op jit(solution)/shard_map/reduce_sum | solution.py:197
Async XLA Ops:
  0.0 8.8 %collective-permute-start = (bf16[3,2,512]{2,1,0:T(2,128)(2,1)}, bf16[3,2,512]{2,1,0:T(2,128)(2,1)S(1)}, u32[]{:S(2)}, u32[]{:S(2)}) collective-permute-start(bf16[3,2,512]{2,1,0:T(2,128)(2,1)} %bitcast.3), channel_id=1, source_target_pairs={{1,0},{2,1},{3,2},{4,3},{5,4},{6,5},{7,6},{8,7},{9,8},{10,9},{11,1... | collective-permute-start | bytes 18440 | tf_op jit(solution)/shard_map/ppermute | solution.py:192

commit v4 on v3

--- a/solution.py
+++ b/solution.py
@@ -54,19 +54,20 @@
 
 def near_kernel(
     live_hbm, own_hbm, template_hbm, moveout_hbm, order_hbm,
-    template_ref, tail_ref, factor_ref, scale_ref, delay_ref, chosen_ref, corner_ref, joined_ref, turned_ref,
-    live_ref, own_ref, moveout_ref, order_ref, frames_ref, small_sem, template_sem, *, gain
+    placed_ref, tail_ref, factor_ref, scale_ref, delay_ref, corner_ref, joined_ref, turned_ref,
+    template_ref, live_ref, own_ref, moveout_ref, order_ref, frames_ref, sems, *, gain
 ):
     components, stations, block = own_ref.shape
     kcount, taps = template_ref.shape[1:]
-    pairs = [(own_hbm, own_ref), (moveout_hbm, moveout_ref), (order_hbm, order_ref), (live_hbm, live_ref)]
-    small = [pltpu.make_async_copy(*pair, small_sem.at[i]) for i, pair in enumerate(pairs)]
-    large = [
-        pltpu.make_async_copy(template_hbm.at[s], template_ref.at[s], template_sem.at[s]) for s in range(stations)
+    pairs = [
+        (own_hbm, own_ref), (moveout_hbm, moveout_ref), (order_hbm, order_ref), (live_hbm, live_ref),
+        (template_hbm, template_ref),
     ]
-    for copy in small + large:
+    copies = [pltpu.make_async_copy(*pair, sems.at[i]) for i, pair in enumerate(pairs)]
+    for copy in copies:
         copy.start()
-    small[0].wait()
+    for copy in copies[:-1]:
+        copy.wait()
     blocks = backwards(own_ref, range(block // LANES))
     rows = jnp.concatenate(blocks, axis=1)
     last = block // LANES - 1
@@ -80,21 +81,23 @@
             for h in range(TLEN // LANES):
                 start = c * TLEN + h * LANES
                 frames_ref[s, start : start + LANES, :] = steps[:, (last - 1 - h) * LANES : (last + 1 - h) * LANES]
-    for copy in small[1:]:
-        copy.wait()
     order = column_of(order_ref[...], kcount)
-    chosen_ref[...] = (order == lax.broadcasted_iota(jnp.int32, (kcount, kcount), 1)).astype(jnp.bfloat16)
-    for s in range(stations):
-        delay_ref[s] = jnp.broadcast_to(column_of(moveout_ref[s : s + 1, :], kcount), (kcount, LANES))
+    chosen = (order == lax.broadcasted_iota(jnp.int32, (kcount, kcount), 1)).astype(jnp.bfloat16)
+    delays = lax.dot_general(
+        chosen, moveout_ref[...].astype(jnp.bfloat16), (((1,), (1,)), ((), ())), preferred_element_type=jnp.float32
+    ).astype(jnp.int32)
+    for s in range(stations):
+        delay_ref[s] = jnp.broadcast_to(delays[:, s : s + 1], (kcount, LANES))
         factor_ref[s] = jnp.broadcast_to(live_ref[0:1, s : s + 1].astype(jnp.float32) * gain, (8, LANES))
-    for s in range(stations):
-        large[s].wait()
+    copies[-1].wait()
+    for s in range(stations):
         record_scale = record_scale_of(rows, stations, s, taps)
-        wide = template_ref[s].astype(jnp.float32)
+        wide = jnp.dot(chosen, template_ref[s], preferred_element_type=jnp.float32)
+        placed_ref[s] = wide.astype(jnp.bfloat16)
         energy = jnp.sum(wide * wide, axis=1, keepdims=True)
         scale = jnp.broadcast_to(1.0 / jnp.sqrt(energy / taps + epsilon), (kcount, LANES))
         scale_ref[s] = scale
-        correlation = jnp.dot(template_ref[s], frames_ref[s], preferred_element_type=jnp.float32)
+        correlation = jnp.dot(placed_ref[s], frames_ref[s], preferred_element_type=jnp.float32)
         reach = lag(delay_ref[s])
         first = turn(block_of(correlation, 1), block_of(record_scale, last), scale, reach)
         second = turn(block_of(correlation, 0), block_of(record_scale, last - 1), scale, reach)
@@ -103,11 +106,11 @@
 
 
 def stack_kernel(
-    next_ref, template_ref, tail_ref, factor_ref, scale_ref, delay_ref, chosen_ref, corner_ref, joined_ref, turned_ref,
+    next_ref, placed_ref, tail_ref, factor_ref, scale_ref, delay_ref, corner_ref, joined_ref, turned_ref,
     out_ref, frames_ref
 ):
     components, stations, block = next_ref.shape
-    kcount, taps = template_ref.shape[1:]
+    kcount, taps = placed_ref.shape[1:]
     count = block // LANES
     rows = jnp.concatenate(backwards(next_ref, range(count)) + [tail_ref[...]], axis=1)
     total = [jnp.zeros((kcount, LANES), jnp.float32) for _ in range(count)]
@@ -121,7 +124,7 @@
             frames_ref[s, start + LANES : start + TLEN, :] = steps[:, LANES:]
     for s in range(stations):
         record_scale = record_scale_of(rows, stations, s, taps)
-        correlation = jnp.dot(template_ref[s], frames_ref[s], preferred_element_type=jnp.float32)
+        correlation = jnp.dot(placed_ref[s], frames_ref[s], preferred_element_type=jnp.float32)
         moveout = delay_ref[s]
         reach = lag(moveout)
         far = moveout >= LANES
@@ -133,9 +136,7 @@
         joined = [joined_ref[s]] + [jnp.where(reach < LANES, turned[i], turned[i + 1]) for i in range(count)]
         for i in range(count):
             total[i] = total[i] + jnp.where(far, joined[i + 1], joined[i]) * factor
-    stacked = jnp.concatenate(total, axis=1).astype(jnp.bfloat16)
-    placed = jnp.dot(chosen_ref[...], stacked, preferred_element_type=jnp.float32)
-    out_ref[...] = placed.astype(jnp.bfloat16).reshape(out_ref.shape)
+    out_ref[...] = jnp.concatenate(total, axis=1).astype(jnp.bfloat16).reshape(out_ref.shape)
 
 
 def near_part(own, templates, moveouts, live_mask, owner_order, gain):
@@ -144,7 +145,7 @@
     row = (stations, kcount, LANES)
     shapes = [
         (templates.shape, jnp.bfloat16), ((-(-components * stations // 8) * 8, 2 * LANES), jnp.float32),
-        ((stations, 8, LANES), jnp.float32), (row, jnp.float32), (row, jnp.int32), ((kcount, kcount), jnp.bfloat16),
+        ((stations, 8, LANES), jnp.float32), (row, jnp.float32), (row, jnp.int32),
         ((stations, taps // 2, LANES), jnp.bfloat16), (row, jnp.float32), (row, jnp.float32),
     ]
     return pl.pallas_call(
@@ -153,13 +154,13 @@
         in_specs=[pl.BlockSpec(memory_space=pltpu.HBM)] * 5,
         out_specs=[pl.BlockSpec(memory_space=pltpu.VMEM)] * len(shapes),
         scratch_shapes=[
+            pltpu.VMEM(templates.shape, templates.dtype),
             pltpu.VMEM((1, stations), jnp.int32),
             pltpu.VMEM(own.shape, own.dtype),
             pltpu.VMEM(moveouts.shape, moveouts.dtype),
             pltpu.VMEM((1, kcount), jnp.int32),
             pltpu.VMEM((stations, taps, 2 * LANES), jnp.bfloat16),
-            pltpu.SemaphoreType.DMA((4,)),
-            pltpu.SemaphoreType.DMA((stations,)),
+            pltpu.SemaphoreType.DMA((5,)),
         ],
         compiler_params=pltpu.CompilerParams(vmem_limit_bytes=32 << 20),
         name="near",

time: 21.2 us -> 21 us (level)
  no operation moved by 1% of the time
where the time goes in v4:
time: 21 us; the launch traced here: 20.8 us
  blocking collectives  10.3 us (49%)
  waiting for transfers between devices  3.83 us (18%)
  Pallas kernels  3.36 us (16%)
  starting transfers between devices  2.57 us (12%)
  other arithmetic  0.67 us (3%)
    all_to_all x1, blocking collectives, shards(): parts = lax.all_to_all(partial, 'sta', 0, 0)  10.3 us
    ppermute x1, waiting for transfers between devices, shards(): lax.ppermute(own, 'tm', [(source, source - 1) for source in range(1, coun...  3.83 us
    ppermute x1, starting transfers between devices, shards(): lax.ppermute(own, 'tm', [(source, source - 1) for source in range(1, coun...  2.57 us
    pallas_call x1, Pallas kernels, near_part(): pl.pallas_call(lambda *refs: near_kernel(*refs, gain=gain), out_shape=[ja...  2.34 us
    pallas_call x1, Pallas kernels, stack_part(): pl.pallas_call(stack_kernel, out_shape=jax.ShapeDtypeStruct((groups, kcou...  1.02 us
    reduce_sum x1, other arithmetic, shards(): return jnp.sum(parts.astype(jnp.float32), axis=0)  0.67 us
  transfers between devices with their start and end apart: 1, of which 1 were waited for; matrix products, arithmetic and copies ran while one was open for 0% of the time, Pallas kernels for 11%

profile of v4, /device:TPU:113, one launch (start us, length us, event | category | flops | bytes accessed | tf_op | source)
XLA Modules:
  0.0 20.8 jit_solution(15278655212463792878)
XLA Ops:
  0.0 2.6 %collective-permute-start = (bf16[3,2,512]{2,1,0:T(2,128)(2,1)}, bf16[3,2,512]{2,1,0:T(2,128)(2,1)S(1)}, u32[]{:S(2)}, u32[]{:S(2)}) collective-permute-start(bf16[3,2,512]{2,1,0:T(2,128)(2,1)} %bitcast.3), channel_id=1, source_target_pairs={{1,0},{2,1},{3,2},{4,3},{5,4},{6,5},{7,6},{8,7},{9,8},{10,9},{11,1... | collective-permute-start | bytes 18440 | tf_op jit(solution)/shard_map/ppermute | solution.py:193
  2.6 2.3 %near.1 = (bf16[2,256,768]{2,1,0:T(8,128)(2,1)S(1)}, f32[8,256]{1,0:T(8,128)S(1)}, f32[2,8,128]{2,1,0:T(8,128)S(1)}, f32[2,256,128]{2,1,0:T(8,128)S(1)}, s32[2,2...) custom-call(s32[1,2]{1,0:T(1,128)} %bitcast.6, ...), custom_call_target="tpu_custom_call" | custom-call | tf_op jit(solution)/shard_map/near/pallas_call | solution.py:151
  4.9 3.8 %collective-permute-done.next_ref = bf16[3,2,512]{2,1,0:T(2,128)(2,1)S(1)} collective-permute-done((bf16[3,2,512]{2,1,0:T(2,128)(2,1)}, bf16[3,2,512]{2,1,0:T(2,128)(2,1)S(1)}, u32[]{:S(2)}, u32[]{:S(2)}) %collective-permute-start) | collective-permute-done | bytes 6176 | tf_op jit(solution)/shard_map/ppermute | solution.py:193
  8.8 1.0 %stack.1 = bf16[8,32,512]{2,1,0:T(8,128)(2,1)S(1)} custom-call(bf16[3,2,512]{2,1,0:T(2,128)(2,1)S(1)} %collective-permute-done.next_ref, bf16[2,256,768]{2,1,0:T(8,128)(2,1)S(1)} %get-tuple-element.13.placed_ref, f32[8,256]{1,0:T(8,128)S(1)} %get-tuple-element.14.tail_ref, f32[2,8,128]{2,1,0:T(8,128)S(1)} %get-tuple-element.15.factor_ref, ...), custom_call_target="tpu_custom_call" | custom-call | tf_op jit(solution)/shard_map/stack/pallas_call | solution.py:177
  9.8 10.3 %all_to_all.5 = bf16[8,32,512]{2,1,0:T(8,128)(2,1)S(1)} all-to-all(bf16[8,32,512]{2,1,0:T(8,128)(2,1)S(1)} %stack.1), channel_id=1, replica_groups=mesh['sta'=8,'tm'=32] {'sta'}, dimensions={0} | all-to-all | bytes 524288 | tf_op jit(solution)/shard_map/all_to_all | solution.py:197
  20.1 0.7 %convert_reduce_fusion = f32[32,512]{1,0:T(8,128)} fusion(bf16[8,32,512]{2,1,0:T(8,128)(2,1)S(1)} %all_to_all.5), kind=kLoop, calls=%fused_computation | loop fusion | flops 245760 | bytes 327680 | tf_op jit(solution)/shard_map/reduce_sum | solution.py:198
Async XLA Ops:
  0.0 8.8 %collective-permute-start = (bf16[3,2,512]{2,1,0:T(2,128)(2,1)}, bf16[3,2,512]{2,1,0:T(2,128)(2,1)S(1)}, u32[]{:S(2)}, u32[]{:S(2)}) collective-permute-start(bf16[3,2,512]{2,1,0:T(2,128)(2,1)} %bitcast.3), channel_id=1, source_target_pairs={{1,0},{2,1},{3,2},{4,3},{5,4},{6,5},{7,6},{8,7},{9,8},{10,9},{11,1... | collective-permute-start | bytes 18440 | tf_op jit(solution)/shard_map/ppermute | solution.py:193

commit v5 on v4

--- a/solution.py
+++ b/solution.py
@@ -64,10 +64,10 @@
         (template_hbm, template_ref),
     ]
     copies = [pltpu.make_async_copy(*pair, sems.at[i]) for i, pair in enumerate(pairs)]
-    for copy in copies:
+    for copy in copies[:1] + copies[2:3] + copies[-1:] + copies[1:2] + copies[3:4]:
         copy.start()
-    for copy in copies[:-1]:
-        copy.wait()
+    copies[0].wait()
+    copies[2].wait()
     blocks = backwards(own_ref, range(block // LANES))
     rows = jnp.concatenate(blocks, axis=1)
     last = block // LANES - 1
@@ -83,13 +83,14 @@
                 frames_ref[s, start : start + LANES, :] = steps[:, (last - 1 - h) * LANES : (last + 1 - h) * LANES]
     order = column_of(order_ref[...], kcount)
     chosen = (order == lax.broadcasted_iota(jnp.int32, (kcount, kcount), 1)).astype(jnp.bfloat16)
+    for copy in (copies[1], copies[3], copies[4]):
+        copy.wait()
     delays = lax.dot_general(
         chosen, moveout_ref[...].astype(jnp.bfloat16), (((1,), (1,)), ((), ())), preferred_element_type=jnp.float32
     ).astype(jnp.int32)
     for s in range(stations):
         delay_ref[s] = jnp.broadcast_to(delays[:, s : s + 1], (kcount, LANES))
         factor_ref[s] = jnp.broadcast_to(live_ref[0:1, s : s + 1].astype(jnp.float32) * gain, (8, LANES))
-    copies[-1].wait()
     for s in range(stations):
         record_scale = record_scale_of(rows, stations, s, taps)
         wide = jnp.dot(chosen, template_ref[s], preferred_element_type=jnp.float32)

time: 21 us -> 21 us (level)
  waiting for transfers between devices: 3.83 us -> 4.11 us
  Pallas kernels: 3.36 us -> 3.08 us
    pallas_call x1, Pallas kernels: 2.34 us -> 2.06 us  [near_part(): pl.pallas_call(lambda *refs: near_kernel(*refs, gain=gain), out_shape=[ja...]
    ppermute x1, waiting for transfers between devices: 3.83 us -> 4.11 us  [shards(): lax.ppermute(own, 'tm', [(source, source - 1) for source in range(1, coun...]
  transfers between devices with their start and end apart: 1 -> 1, of which waited for: 1 -> 1; matrix products, arithmetic and copies ran while one was open for 0% -> 0% of each run, Pallas kernels for 11% -> 10%
where the time goes in v5:
time: 21 us; the launch traced here: 20.8 us
  blocking collectives  10.3 us (49%)
  waiting for transfers between devices  4.11 us (20%)
  Pallas kernels  3.08 us (15%)
  starting transfers between devices  2.57 us (12%)
  other arithmetic  0.67 us (3%)
    all_to_all x1, blocking collectives, shards(): parts = lax.all_to_all(partial, 'sta', 0, 0)  10.3 us
    ppermute x1, waiting for transfers between devices, shards(): lax.ppermute(own, 'tm', [(source, source - 1) for source in range(1, coun...  4.11 us
    ppermute x1, starting transfers between devices, shards(): lax.ppermute(own, 'tm', [(source, source - 1) for source in range(1, coun...  2.57 us
    pallas_call x1, Pallas kernels, near_part(): pl.pallas_call(lambda *refs: near_kernel(*refs, gain=gain), out_shape=[ja...  2.06 us
    pallas_call x1, Pallas kernels, stack_part(): pl.pallas_call(stack_kernel, out_shape=jax.ShapeDtypeStruct((groups, kcou...  1.02 us
    reduce_sum x1, other arithmetic, shards(): return jnp.sum(parts.astype(jnp.float32), axis=0)  0.67 us
  transfers between devices with their start and end apart: 1, of which 1 were waited for; matrix products, arithmetic and copies ran while one was open for 0% of the time, Pallas kernels for 10%

profile of v5, /device:TPU:113, one launch (start us, length us, event | category | flops | bytes accessed | tf_op | source)
XLA Modules:
  0.0 20.8 jit_solution(10980636090874864111)
XLA Ops:
  0.0 2.6 %collective-permute-start = (bf16[3,2,512]{2,1,0:T(2,128)(2,1)}, bf16[3,2,512]{2,1,0:T(2,128)(2,1)S(1)}, u32[]{:S(2)}, u32[]{:S(2)}) collective-permute-start(bf16[3,2,512]{2,1,0:T(2,128)(2,1)} %bitcast.3), channel_id=1, source_target_pairs={{1,0},{2,1},{3,2},{4,3},{5,4},{6,5},{7,6},{8,7},{9,8},{10,9},{11,1... | collective-permute-start | bytes 18440 | tf_op jit(solution)/shard_map/ppermute | solution.py:194
  2.6 2.1 %near.1 = (bf16[2,256,768]{2,1,0:T(8,128)(2,1)S(1)}, f32[8,256]{1,0:T(8,128)S(1)}, f32[2,8,128]{2,1,0:T(8,128)S(1)}, f32[2,256,128]{2,1,0:T(8,128)S(1)}, s32[2,2...) custom-call(s32[1,2]{1,0:T(1,128)} %bitcast.6, ...), custom_call_target="tpu_custom_call" | custom-call | tf_op jit(solution)/shard_map/near/pallas_call | solution.py:152
  4.6 4.1 %collective-permute-done.next_ref = bf16[3,2,512]{2,1,0:T(2,128)(2,1)S(1)} collective-permute-done((bf16[3,2,512]{2,1,0:T(2,128)(2,1)}, bf16[3,2,512]{2,1,0:T(2,128)(2,1)S(1)}, u32[]{:S(2)}, u32[]{:S(2)}) %collective-permute-start) | collective-permute-done | bytes 6176 | tf_op jit(solution)/shard_map/ppermute | solution.py:194
  8.8 1.0 %stack.1 = bf16[8,32,512]{2,1,0:T(8,128)(2,1)S(1)} custom-call(bf16[3,2,512]{2,1,0:T(2,128)(2,1)S(1)} %collective-permute-done.next_ref, bf16[2,256,768]{2,1,0:T(8,128)(2,1)S(1)} %get-tuple-element.13.placed_ref, f32[8,256]{1,0:T(8,128)S(1)} %get-tuple-element.14.tail_ref, f32[2,8,128]{2,1,0:T(8,128)S(1)} %get-tuple-element.15.factor_ref, ...), custom_call_target="tpu_custom_call" | custom-call | tf_op jit(solution)/shard_map/stack/pallas_call | solution.py:178
  9.8 10.3 %all_to_all.5 = bf16[8,32,512]{2,1,0:T(8,128)(2,1)S(1)} all-to-all(bf16[8,32,512]{2,1,0:T(8,128)(2,1)S(1)} %stack.1), channel_id=1, replica_groups=mesh['sta'=8,'tm'=32] {'sta'}, dimensions={0} | all-to-all | bytes 524288 | tf_op jit(solution)/shard_map/all_to_all | solution.py:198
  20.1 0.7 %convert_reduce_fusion = f32[32,512]{1,0:T(8,128)} fusion(bf16[8,32,512]{2,1,0:T(8,128)(2,1)S(1)} %all_to_all.5), kind=kLoop, calls=%fused_computation | loop fusion | flops 245760 | bytes 327680 | tf_op jit(solution)/shard_map/reduce_sum | solution.py:199
Async XLA Ops:
  0.0 8.8 %collective-permute-start = (bf16[3,2,512]{2,1,0:T(2,128)(2,1)}, bf16[3,2,512]{2,1,0:T(2,128)(2,1)S(1)}, u32[]{:S(2)}, u32[]{:S(2)}) collective-permute-start(bf16[3,2,512]{2,1,0:T(2,128)(2,1)} %bitcast.3), channel_id=1, source_target_pairs={{1,0},{2,1},{3,2},{4,3},{5,4},{6,5},{7,6},{8,7},{9,8},{10,9},{11,1... | collective-permute-start | bytes 18440 | tf_op jit(solution)/shard_map/ppermute | solution.py:194

commit v6 on v5

--- a/solution.py
+++ b/solution.py
@@ -113,7 +113,8 @@
     components, stations, block = next_ref.shape
     kcount, taps = placed_ref.shape[1:]
     count = block // LANES
-    rows = jnp.concatenate(backwards(next_ref, range(count)) + [tail_ref[...]], axis=1)
+    inside = (lax.axis_index("tm") < lax.axis_size("tm") - 1).astype(jnp.float32)
+    rows = jnp.concatenate([part * inside for part in backwards(next_ref, range(count))] + [tail_ref[...]], axis=1)
     total = [jnp.zeros((kcount, LANES), jnp.float32) for _ in range(count)]
     for s in range(stations):
         for c in range(components):
@@ -191,7 +192,7 @@
     count = lax.axis_size("tm")
     groups = lax.axis_size("sta")
     own = jnp.transpose(record, (1, 0, 2))
-    ahead = lax.ppermute(own, "tm", [(source, source - 1) for source in range(1, count)])
+    ahead = lax.ppermute(own, "tm", [(source, (source - 1) % count) for source in range(count)])
     gain = math.sqrt(components * TLEN / (stations * groups))
     near = near_part(own, templates, moveouts, live_mask, owner_order, gain)
     partial = stack_part(ahead, near, groups)

time: 21 us -> 22.6 us (1.076)
  the two profiles are of different devices: /device:TPU:113 before, /device:TPU:8 now
where the time goes in v6:
time: 22.6 us; the launch traced here: 22.5 us
  blocking collectives  11.7 us (52%)
  starting transfers between devices  7.03 us (31%)
  Pallas kernels  3.08 us (14%)
  other arithmetic  0.67 us (3%)
    all_to_all x1, blocking collectives, shards(): parts = lax.all_to_all(partial, 'sta', 0, 0)  11.7 us
    ppermute x1, starting transfers between devices, shards(): lax.ppermute(own, 'tm', [(source, (source - 1) % count) for source in ran...  7.03 us
    pallas_call x1, Pallas kernels, near_part(): pl.pallas_call(lambda *refs: near_kernel(*refs, gain=gain), out_shape=[ja...  2.07 us
    pallas_call x1, Pallas kernels, stack_part(): pl.pallas_call(stack_kernel, out_shape=jax.ShapeDtypeStruct((groups, kcou...  1.01 us
    reduce_sum x1, other arithmetic, shards(): return jnp.sum(parts.astype(jnp.float32), axis=0)  0.67 us
  transfers between devices with their start and end apart: 1, of which 0 were waited for; matrix products, arithmetic and copies ran while one was open for 0% of the time, Pallas kernels for 9%

profile of v6, /device:TPU:8, one launch (start us, length us, event | category | flops | bytes accessed | tf_op | source)
XLA Modules:
  0.0 22.5 jit_solution(6983060488859308813)
XLA Ops:
  0.0 7.0 %collective-permute-start = (bf16[3,2,512]{2,1,0:T(2,128)(2,1)}, bf16[3,2,512]{2,1,0:T(2,128)(2,1)S(1)}, u32[]{:S(2)}, u32[]{:S(2)}) collective-permute-start(bf16[3,2,512]{2,1,0:T(2,128)(2,1)} %bitcast.3), channel_id=1, source_target_pairs={{0,31},{1,0},{2,1},{3,2},{4,3},{5,4},{6,5},{7,6},{8,7},{9,8},{10,9... | collective-permute-start | bytes 18440 | tf_op jit(solution)/shard_map/ppermute | solution.py:195
  7.0 2.1 %near.1 = (bf16[2,256,768]{2,1,0:T(8,128)(2,1)S(1)}, f32[8,256]{1,0:T(8,128)S(1)}, f32[2,8,128]{2,1,0:T(8,128)S(1)}, f32[2,256,128]{2,1,0:T(8,128)S(1)}, s32[2,2...) custom-call(s32[1,2]{1,0:T(1,128)} %bitcast.6, ...), custom_call_target="tpu_custom_call" | custom-call | tf_op jit(solution)/shard_map/near/pallas_call | solution.py:153
  9.1 0.0 collective-permute-done.next_ref
  9.1 1.0 %stack.1 = bf16[8,32,512]{2,1,0:T(8,128)(2,1)S(1)} custom-call(bf16[3,2,512]{2,1,0:T(2,128)(2,1)S(1)} %collective-permute-done.next_ref, bf16[2,256,768]{2,1,0:T(8,128)(2,1)S(1)} %get-tuple-element.13.placed_ref, f32[8,256]{1,0:T(8,128)S(1)} %get-tuple-element.14.tail_ref, f32[2,8,128]{2,1,0:T(8,128)S(1)} %get-tuple-element.15.factor_ref, ...), custom_call_target="tpu_custom_call" | custom-call | tf_op jit(solution)/shard_map/stack/pallas_call | solution.py:179
  10.1 11.7 %all_to_all.5 = bf16[8,32,512]{2,1,0:T(8,128)(2,1)S(1)} all-to-all(bf16[8,32,512]{2,1,0:T(8,128)(2,1)S(1)} %stack.1), channel_id=1, replica_groups=mesh['sta'=8,'tm'=32] {'sta'}, dimensions={0} | all-to-all | bytes 524288 | tf_op jit(solution)/shard_map/all_to_all | solution.py:199
  21.8 0.7 %convert_reduce_fusion = f32[32,512]{1,0:T(8,128)} fusion(bf16[8,32,512]{2,1,0:T(8,128)(2,1)S(1)} %all_to_all.5), kind=kLoop, calls=%fused_computation | loop fusion | flops 245760 | bytes 327680 | tf_op jit(solution)/shard_map/reduce_sum | solution.py:200
Async XLA Ops:
  0.0 9.1 %collective-permute-start = (bf16[3,2,512]{2,1,0:T(2,128)(2,1)}, bf16[3,2,512]{2,1,0:T(2,128)(2,1)S(1)}, u32[]{:S(2)}, u32[]{:S(2)}) collective-permute-start(bf16[3,2,512]{2,1,0:T(2,128)(2,1)} %bitcast.3), channel_id=1, source_target_pairs={{0,31},{1,0},{2,1},{3,2},{4,3},{5,4},{6,5},{7,6},{8,7},{9,8},{10,9... | collective-permute-start | bytes 18440 | tf_op jit(solution)/shard_map/ppermute | solution.py:195

commit v7 on v5

--- a/solution.py
+++ b/solution.py
@@ -107,13 +107,17 @@
 
 
 def stack_kernel(
-    next_ref, placed_ref, tail_ref, factor_ref, scale_ref, delay_ref, corner_ref, joined_ref, turned_ref,
+    chip_ref, next_ref, placed_ref, tail_ref, factor_ref, scale_ref, delay_ref, corner_ref, joined_ref, turned_ref,
     out_ref, frames_ref
 ):
     components, stations, block = next_ref.shape
     kcount, taps = placed_ref.shape[1:]
     count = block // LANES
-    rows = jnp.concatenate(backwards(next_ref, range(count)) + [tail_ref[...]], axis=1)
+    place = lax.axis_index("tm")
+    even = (place % 2 == 0).astype(jnp.float32)
+    odd = (1.0 - even) * (place < lax.axis_size("tm") - 1).astype(jnp.float32)
+    arrived = zip(backwards(chip_ref, range(count)), backwards(next_ref, range(count)))
+    rows = jnp.concatenate([near * even + far * odd for near, far in arrived] + [tail_ref[...]], axis=1)
     total = [jnp.zeros((kcount, LANES), jnp.float32) for _ in range(count)]
     for s in range(stations):
         for c in range(components):
@@ -172,18 +176,25 @@
 
 
 def stack_part(ahead, near, groups):
-    components, stations, block = ahead.shape
+    components, stations, block = ahead[0].shape
     kcount, taps = near[0].shape[1:]
     vmem = pl.BlockSpec(memory_space=pltpu.VMEM)
     return pl.pallas_call(
         stack_kernel,
         out_shape=jax.ShapeDtypeStruct((groups, kcount // groups, block), jnp.bfloat16),
-        in_specs=[vmem] * (1 + len(near)),
+        in_specs=[vmem] * (len(ahead) + len(near)),
         out_specs=vmem,
         scratch_shapes=[pltpu.VMEM((stations, taps, block), jnp.bfloat16)],
         compiler_params=pltpu.CompilerParams(vmem_limit_bytes=32 << 20),
         name="stack",
-    )(ahead, *near)
+    )(*ahead, *near)
+
+
+def swaps(count, first):
+    pairs = [(i, i) for i in range(count)]
+    for i in range(first, count - 1, 2):
+        pairs[i], pairs[i + 1] = (i, i + 1), (i + 1, i)
+    return pairs
 
 
 def shards(record, templates, moveouts, live_mask, owner_order):
@@ -191,7 +202,7 @@
     count = lax.axis_size("tm")
     groups = lax.axis_size("sta")
     own = jnp.transpose(record, (1, 0, 2))
-    ahead = lax.ppermute(own, "tm", [(source, source - 1) for source in range(1, count)])
+    ahead = (lax.ppermute(own, "tm", swaps(count, 0)), lax.ppermute(own, "tm", swaps(count, 1)))
     gain = math.sqrt(components * TLEN / (stations * groups))
     near = near_part(own, templates, moveouts, live_mask, owner_order, gain)
     partial = stack_part(ahead, near, groups)

time: 21 us -> 22.7 us (1.081)
  the two profiles are of different devices: /device:TPU:113 before, /device:TPU:128 now
where the time goes in v7:
time: 22.7 us; the launch traced here: 22.5 us
  blocking collectives  12 us (53%)
  starting transfers between devices  5.29 us (23%)
  Pallas kernels  3.08 us (14%)
  waiting for transfers between devices  1.4 us (6%)
  other arithmetic  0.67 us (3%)
    all_to_all x1, blocking collectives, shards(): parts = lax.all_to_all(partial, 'sta', 0, 0)  12 us
    ppermute x1, starting transfers between devices, shards(): lax.ppermute(own, 'tm', swaps(count, 1))  4.07 us
    pallas_call x1, Pallas kernels, near_part(): pl.pallas_call(lambda *refs: near_kernel(*refs, gain=gain), out_shape=[ja...  2.06 us
    ppermute x1, waiting for transfers between devices, shards(): lax.ppermute(own, 'tm', swaps(count, 1))  1.39 us
    ppermute x1, starting transfers between devices, shards(): lax.ppermute(own, 'tm', swaps(count, 0))  1.22 us
    pallas_call x1, Pallas kernels, stack_part(): pl.pallas_call(stack_kernel, out_shape=jax.ShapeDtypeStruct((groups, kcou...  1.02 us
    reduce_sum x1, other arithmetic, shards(): return jnp.sum(parts.astype(jnp.float32), axis=0)  0.67 us
  transfers between devices with their start and end apart: 2, of which 1 were waited for; matrix products, arithmetic and copies ran while one was open for 0% of the time, Pallas kernels for 9%

profile of v7, /device:TPU:128, one launch (start us, length us, event | category | flops | bytes accessed | tf_op | source)
XLA Modules:
  0.0 22.5 jit_solution(4342688755634940239)
XLA Ops:
  0.0 4.1 %collective-permute-start.1 = (bf16[3,2,512]{2,1,0:T(2,128)(2,1)}, bf16[3,2,512]{2,1,0:T(2,128)(2,1)S(1)}, u32[]{:S(2)}, u32[]{:S(2)}) collective-permute-start(bf16[3,2,512]{2,1,0:T(2,128)(2,1)} %bitcast.3), channel_id=1, source_target_pairs={{0,0},{1,2},{2,1},{3,4},{4,3},{5,6},{6,5},{7,8},{8,7},{9,10},{10,9... | collective-permute-start | bytes 18440 | tf_op jit(solution)/shard_map/ppermute | solution.py:205
  4.1 1.2 %collective-permute-start = (bf16[3,2,512]{2,1,0:T(2,128)(2,1)}, bf16[3,2,512]{2,1,0:T(2,128)(2,1)S(1)}, u32[]{:S(2)}, u32[]{:S(2)}) collective-permute-start(bf16[3,2,512]{2,1,0:T(2,128)(2,1)} %bitcast.4), channel_id=1, source_target_pairs={{0,1},{1,0},{2,3},{3,2},{4,5},{5,4},{6,7},{7,6},{8,9},{9,8},{10,11... | collective-permute-start | bytes 18440 | tf_op jit(solution)/shard_map/ppermute | solution.py:205
  5.3 2.1 %near.1 = (bf16[2,256,768]{2,1,0:T(8,128)(2,1)S(1)}, f32[8,256]{1,0:T(8,128)S(1)}, f32[2,8,128]{2,1,0:T(8,128)S(1)}, f32[2,256,128]{2,1,0:T(8,128)S(1)}, s32[2,2...) custom-call(s32[1,2]{1,0:T(1,128)} %bitcast.7, ...), custom_call_target="tpu_custom_call" | custom-call | tf_op jit(solution)/shard_map/near/pallas_call | solution.py:156
  7.4 1.4 %collective-permute-done.1.next_ref = bf16[3,2,512]{2,1,0:T(2,128)(2,1)S(1)} collective-permute-done((bf16[3,2,512]{2,1,0:T(2,128)(2,1)}, bf16[3,2,512]{2,1,0:T(2,128)(2,1)S(1)}, u32[]{:S(2)}, u32[]{:S(2)}) %collective-permute-start.1) | collective-permute-done | bytes 6176 | tf_op jit(solution)/shard_map/ppermute | solution.py:205
  8.8 0.0 collective-permute-done.chip_ref
  8.8 1.0 %stack.1 = bf16[8,32,512]{2,1,0:T(8,128)(2,1)S(1)} custom-call(bf16[3,2,512]{2,1,0:T(2,128)(2,1)S(1)} %collective-permute-done.chip_ref, bf16[3,2,512]{2,1,0:T(2,128)(2,1)S(1)} %collective-permute-done.1.next_ref, bf16[2,256,768]{2,1,0:T(8,128)(2,1)S(1)} %get-tuple-element.13.placed_ref, f32[8,256]{1,0:T(8,128)S(1)} %get-tuple-element.14.tail_ref, ...), custom_call_target="tpu_custom_call" | custom-call | tf_op jit(solution)/shard_map/stack/pallas_call | solution.py:182
  9.8 12.0 %all_to_all.5 = bf16[8,32,512]{2,1,0:T(8,128)(2,1)S(1)} all-to-all(bf16[8,32,512]{2,1,0:T(8,128)(2,1)S(1)} %stack.1), channel_id=1, replica_groups=mesh['sta'=8,'tm'=32] {'sta'}, dimensions={0} | all-to-all | bytes 524288 | tf_op jit(solution)/shard_map/all_to_all | solution.py:209
  21.8 0.7 %convert_reduce_fusion = f32[32,512]{1,0:T(8,128)} fusion(bf16[8,32,512]{2,1,0:T(8,128)(2,1)S(1)} %all_to_all.5), kind=kLoop, calls=%fused_computation | loop fusion | flops 245760 | bytes 327680 | tf_op jit(solution)/shard_map/reduce_sum | solution.py:210
Async XLA Ops:
  0.0 8.8 %collective-permute-start.1 = (bf16[3,2,512]{2,1,0:T(2,128)(2,1)}, bf16[3,2,512]{2,1,0:T(2,128)(2,1)S(1)}, u32[]{:S(2)}, u32[]{:S(2)}) collective-permute-start(bf16[3,2,512]{2,1,0:T(2,128)(2,1)} %bitcast.3), channel_id=1, source_target_pairs={{0,0},{1,2},{2,1},{3,4},{4,3},{5,6},{6,5},{7,8},{8,7},{9,10},{10,9... | collective-permute-start | bytes 18440 | tf_op jit(solution)/shard_map/ppermute | solution.py:205
  4.1 4.7 %collective-permute-start = (bf16[3,2,512]{2,1,0:T(2,128)(2,1)}, bf16[3,2,512]{2,1,0:T(2,128)(2,1)S(1)}, u32[]{:S(2)}, u32[]{:S(2)}) collective-permute-start(bf16[3,2,512]{2,1,0:T(2,128)(2,1)} %bitcast.4), channel_id=1, source_target_pairs={{0,1},{1,0},{2,3},{3,2},{4,5},{5,4},{6,7},{7,6},{8,9},{9,8},{10,11... | collective-permute-start | bytes 18440 | tf_op jit(solution)/shard_map/ppermute | solution.py:205

commit v8 on v7

--- a/solution.py
+++ b/solution.py
@@ -191,10 +191,13 @@
 
 
 def swaps(count, first):
-    pairs = [(i, i) for i in range(count)]
+    pairs = {}
     for i in range(first, count - 1, 2):
-        pairs[i], pairs[i + 1] = (i, i + 1), (i + 1, i)
-    return pairs
+        pairs[i], pairs[i + 1] = i + 1, i
+    if first:
+        end = count - 1
+        pairs.update({0: 2, 1: 0, end: end - 1, end - 2: end})
+    return list(pairs.items())
 
 
 def shards(record, templates, moveouts, live_mask, owner_order):

time: 22.7 us -> 20.8 us (0.916)
  starting transfers between devices: 5.29 us -> 3.31 us
    ppermute x1, starting transfers between devices: 4.07 us -> 2.18 us  [shards(): lax.ppermute(own, 'tm', swaps(count, 1))]
  transfers between devices with their start and end apart: 2 -> 2, of which waited for: 1 -> 1; matrix products, arithmetic and copies ran while one was open for 0% -> 0% of each run, Pallas kernels for 9% -> 10%
where the time goes in v8:
time: 20.8 us; the launch traced here: 20.6 us
  blocking collectives  12 us (58%)
  starting transfers between devices  3.31 us (16%)
  Pallas kernels  3.08 us (15%)
  waiting for transfers between devices  1.5 us (7%)
  other arithmetic  0.67 us (3%)
    all_to_all x1, blocking collectives, shards(): parts = lax.all_to_all(partial, 'sta', 0, 0)  12 us
    ppermute x1, starting transfers between devices, shards(): lax.ppermute(own, 'tm', swaps(count, 1))  2.18 us
    pallas_call x1, Pallas kernels, near_part(): pl.pallas_call(lambda *refs: near_kernel(*refs, gain=gain), out_shape=[ja...  2.06 us
    ppermute x1, waiting for transfers between devices, shards(): lax.ppermute(own, 'tm', swaps(count, 1))  1.5 us
    ppermute x1, starting transfers between devices, shards(): lax.ppermute(own, 'tm', swaps(count, 0))  1.13 us
    pallas_call x1, Pallas kernels, stack_part(): pl.pallas_call(stack_kernel, out_shape=jax.ShapeDtypeStruct((groups, kcou...  1.02 us
    reduce_sum x1, other arithmetic, shards(): return jnp.sum(parts.astype(jnp.float32), axis=0)  0.67 us
  transfers between devices with their start and end apart: 2, of which 1 were waited for; matrix products, arithmetic and copies ran while one was open for 0% of the time, Pallas kernels for 10%

profile of v8, /device:TPU:128, one launch (start us, length us, event | category | flops | bytes accessed | tf_op | source)
XLA Modules:
  0.0 20.6 jit_solution(14780291041658591809)
XLA Ops:
  0.0 2.2 %collective-permute-start.1 = (bf16[3,2,512]{2,1,0:T(2,128)(2,1)}, bf16[3,2,512]{2,1,0:T(2,128)(2,1)S(1)}, u32[]{:S(2)}, u32[]{:S(2)}) collective-permute-start(bf16[3,2,512]{2,1,0:T(2,128)(2,1)} %bitcast.3), channel_id=1, source_target_pairs={{1,0},{2,1},{3,4},{4,3},{5,6},{6,5},{7,8},{8,7},{9,10},{10,9},{11,... | collective-permute-start | bytes 18440 | tf_op jit(solution)/shard_map/ppermute | solution.py:208
  2.2 1.1 %collective-permute-start = (bf16[3,2,512]{2,1,0:T(2,128)(2,1)}, bf16[3,2,512]{2,1,0:T(2,128)(2,1)S(1)}, u32[]{:S(2)}, u32[]{:S(2)}) collective-permute-start(bf16[3,2,512]{2,1,0:T(2,128)(2,1)} %bitcast.4), channel_id=1, source_target_pairs={{0,1},{1,0},{2,3},{3,2},{4,5},{5,4},{6,7},{7,6},{8,9},{9,8},{10,11... | collective-permute-start | bytes 18440 | tf_op jit(solution)/shard_map/ppermute | solution.py:208
  3.3 2.1 %near.1 = (bf16[2,256,768]{2,1,0:T(8,128)(2,1)S(1)}, f32[8,256]{1,0:T(8,128)S(1)}, f32[2,8,128]{2,1,0:T(8,128)S(1)}, f32[2,256,128]{2,1,0:T(8,128)S(1)}, s32[2,2...) custom-call(s32[1,2]{1,0:T(1,128)} %bitcast.7, ...), custom_call_target="tpu_custom_call" | custom-call | tf_op jit(solution)/shard_map/near/pallas_call | solution.py:156
  5.4 1.5 %collective-permute-done.1.next_ref = bf16[3,2,512]{2,1,0:T(2,128)(2,1)S(1)} collective-permute-done((bf16[3,2,512]{2,1,0:T(2,128)(2,1)}, bf16[3,2,512]{2,1,0:T(2,128)(2,1)S(1)}, u32[]{:S(2)}, u32[]{:S(2)}) %collective-permute-start.1) | collective-permute-done | bytes 6176 | tf_op jit(solution)/shard_map/ppermute | solution.py:208
  6.9 0.0 collective-permute-done.chip_ref
  6.9 1.0 %stack.1 = bf16[8,32,512]{2,1,0:T(8,128)(2,1)S(1)} custom-call(bf16[3,2,512]{2,1,0:T(2,128)(2,1)S(1)} %collective-permute-done.chip_ref, bf16[3,2,512]{2,1,0:T(2,128)(2,1)S(1)} %collective-permute-done.1.next_ref, bf16[2,256,768]{2,1,0:T(8,128)(2,1)S(1)} %get-tuple-element.13.placed_ref, f32[8,256]{1,0:T(8,128)S(1)} %get-tuple-element.14.tail_ref, ...), custom_call_target="tpu_custom_call" | custom-call | tf_op jit(solution)/shard_map/stack/pallas_call | solution.py:182
  7.9 12.0 %all_to_all.5 = bf16[8,32,512]{2,1,0:T(8,128)(2,1)S(1)} all-to-all(bf16[8,32,512]{2,1,0:T(8,128)(2,1)S(1)} %stack.1), channel_id=1, replica_groups=mesh['sta'=8,'tm'=32] {'sta'}, dimensions={0} | all-to-all | bytes 524288 | tf_op jit(solution)/shard_map/all_to_all | solution.py:212
  20.0 0.7 %convert_reduce_fusion = f32[32,512]{1,0:T(8,128)} fusion(bf16[8,32,512]{2,1,0:T(8,128)(2,1)S(1)} %all_to_all.5), kind=kLoop, calls=%fused_computation | loop fusion | flops 245760 | bytes 327680 | tf_op jit(solution)/shard_map/reduce_sum | solution.py:213
Async XLA Ops:
  0.0 6.9 %collective-permute-start.1 = (bf16[3,2,512]{2,1,0:T(2,128)(2,1)}, bf16[3,2,512]{2,1,0:T(2,128)(2,1)S(1)}, u32[]{:S(2)}, u32[]{:S(2)}) collective-permute-start(bf16[3,2,512]{2,1,0:T(2,128)(2,1)} %bitcast.3), channel_id=1, source_target_pairs={{1,0},{2,1},{3,4},{4,3},{5,6},{6,5},{7,8},{8,7},{9,10},{10,9},{11,... | collective-permute-start | bytes 18440 | tf_op jit(solution)/shard_map/ppermute | solution.py:208
  2.2 4.7 %collective-permute-start = (bf16[3,2,512]{2,1,0:T(2,128)(2,1)}, bf16[3,2,512]{2,1,0:T(2,128)(2,1)S(1)}, u32[]{:S(2)}, u32[]{:S(2)}) collective-permute-start(bf16[3,2,512]{2,1,0:T(2,128)(2,1)} %bitcast.4), channel_id=1, source_target_pairs={{0,1},{1,0},{2,3},{3,2},{4,5},{5,4},{6,7},{7,6},{8,9},{9,8},{10,11... | collective-permute-start | bytes 18440 | tf_op jit(solution)/shard_map/ppermute | solution.py:208

commit v9 on v7

--- a/solution.py
+++ b/solution.py
@@ -114,10 +114,10 @@
     kcount, taps = placed_ref.shape[1:]
     count = block // LANES
     place = lax.axis_index("tm")
-    even = (place % 2 == 0).astype(jnp.float32)
-    odd = (1.0 - even) * (place < lax.axis_size("tm") - 1).astype(jnp.float32)
+    near = (place % 4 == 0).astype(jnp.float32)
+    far = (1.0 - near) * (place < lax.axis_size("tm") - 1).astype(jnp.float32)
     arrived = zip(backwards(chip_ref, range(count)), backwards(next_ref, range(count)))
-    rows = jnp.concatenate([near * even + far * odd for near, far in arrived] + [tail_ref[...]], axis=1)
+    rows = jnp.concatenate([chip * near + other * far for chip, other in arrived] + [tail_ref[...]], axis=1)
     total = [jnp.zeros((kcount, LANES), jnp.float32) for _ in range(count)]
     for s in range(stations):
         for c in range(components):
@@ -190,11 +190,15 @@
     )(*ahead, *near)
 
 
-def swaps(count, first):
-    pairs = [(i, i) for i in range(count)]
-    for i in range(first, count - 1, 2):
-        pairs[i], pairs[i + 1] = (i, i + 1), (i + 1, i)
-    return pairs
+def swapped(count):
+    return [(i, i ^ 1) for i in range(count)]
+
+
+def backward(count):
+    pairs = {i: i - 1 for i in range(1, count)}
+    pairs.update({i: i + 3 for i in range(5, count - 3, 4)})
+    pairs.update({0: 4, count - 3: count - 1})
+    return list(pairs.items())
 
 
 def shards(record, templates, moveouts, live_mask, owner_order):
@@ -202,7 +206,7 @@
     count = lax.axis_size("tm")
     groups = lax.axis_size("sta")
     own = jnp.transpose(record, (1, 0, 2))
-    ahead = (lax.ppermute(own, "tm", swaps(count, 0)), lax.ppermute(own, "tm", swaps(count, 1)))
+    ahead = (lax.ppermute(own, "tm", swapped(count)), lax.ppermute(own, "tm", backward(count)))
     gain = math.sqrt(components * TLEN / (stations * groups))
     near = near_part(own, templates, moveouts, live_mask, owner_order, gain)
     partial = stack_part(ahead, near, groups)

time: 22.7 us -> 19.6 us (0.86)
  the two profiles are of different devices: /device:TPU:128 before, /device:TPU:96 now
where the time goes in v9:
time: 19.6 us; the launch traced here: 19.4 us
  blocking collectives  12.4 us (63%)
  starting transfers between devices  3.24 us (17%)
  Pallas kernels  3.07 us (16%)
  other arithmetic  0.67 us (3%)
    all_to_all x1, blocking collectives, shards(): parts = lax.all_to_all(partial, 'sta', 0, 0)  12.4 us
    ppermute x1, starting transfers between devices, shards(): lax.ppermute(own, 'tm', backward(count))  2.18 us
    pallas_call x1, Pallas kernels, near_part(): pl.pallas_call(lambda *refs: near_kernel(*refs, gain=gain), out_shape=[ja...  2.06 us
    ppermute x1, starting transfers between devices, shards(): lax.ppermute(own, 'tm', swapped(count))  1.06 us
    pallas_call x1, Pallas kernels, stack_part(): pl.pallas_call(stack_kernel, out_shape=jax.ShapeDtypeStruct((groups, kcou...  1.01 us
    reduce_sum x1, other arithmetic, shards(): return jnp.sum(parts.astype(jnp.float32), axis=0)  0.67 us
  transfers between devices with their start and end apart: 2, of which 0 were waited for; matrix products, arithmetic and copies ran while one was open for 0% of the time, Pallas kernels for 11%

profile of v9, /device:TPU:96, one launch (start us, length us, event | category | flops | bytes accessed | tf_op | source)
XLA Modules:
  0.0 19.4 jit_solution(7082412534558432279)
XLA Ops:
  0.0 2.2 %collective-permute-start.1 = (bf16[3,2,512]{2,1,0:T(2,128)(2,1)}, bf16[3,2,512]{2,1,0:T(2,128)(2,1)S(1)}, u32[]{:S(2)}, u32[]{:S(2)}) collective-permute-start(bf16[3,2,512]{2,1,0:T(2,128)(2,1)} %bitcast.3), channel_id=1, source_target_pairs={{1,0},{2,1},{3,2},{4,3},{5,8},{6,5},{7,6},{8,7},{9,12},{10,9},{11,... | collective-permute-start | bytes 18440 | tf_op jit(solution)/shard_map/ppermute | solution.py:209
  2.2 1.1 %collective-permute-start = (bf16[3,2,512]{2,1,0:T(2,128)(2,1)}, bf16[3,2,512]{2,1,0:T(2,128)(2,1)S(1)}, u32[]{:S(2)}, u32[]{:S(2)}) collective-permute-start(bf16[3,2,512]{2,1,0:T(2,128)(2,1)} %bitcast.4), channel_id=1, source_target_pairs={{0,1},{1,0},{2,3},{3,2},{4,5},{5,4},{6,7},{7,6},{8,9},{9,8},{10,11... | collective-permute-start | bytes 18440 | tf_op jit(solution)/shard_map/ppermute | solution.py:209
  3.2 2.1 %near.1 = (bf16[2,256,768]{2,1,0:T(8,128)(2,1)S(1)}, f32[8,256]{1,0:T(8,128)S(1)}, f32[2,8,128]{2,1,0:T(8,128)S(1)}, f32[2,256,128]{2,1,0:T(8,128)S(1)}, s32[2,2...) custom-call(s32[1,2]{1,0:T(1,128)} %bitcast.7, ...), custom_call_target="tpu_custom_call" | custom-call | tf_op jit(solution)/shard_map/near/pallas_call | solution.py:156
  5.3 0.0 collective-permute-done.1.next_ref
  5.3 0.0 collective-permute-done.chip_ref
  5.3 1.0 %stack.1 = bf16[8,32,512]{2,1,0:T(8,128)(2,1)S(1)} custom-call(bf16[3,2,512]{2,1,0:T(2,128)(2,1)S(1)} %collective-permute-done.chip_ref, bf16[3,2,512]{2,1,0:T(2,128)(2,1)S(1)} %collective-permute-done.1.next_ref, bf16[2,256,768]{2,1,0:T(8,128)(2,1)S(1)} %get-tuple-element.13.placed_ref, f32[8,256]{1,0:T(8,128)S(1)} %get-tuple-element.14.tail_ref, ...), custom_call_target="tpu_custom_call" | custom-call | tf_op jit(solution)/shard_map/stack/pallas_call | solution.py:182
  6.4 12.4 %all_to_all.5 = bf16[8,32,512]{2,1,0:T(8,128)(2,1)S(1)} all-to-all(bf16[8,32,512]{2,1,0:T(8,128)(2,1)S(1)} %stack.1), channel_id=1, replica_groups=mesh['sta'=8,'tm'=32] {'sta'}, dimensions={0} | all-to-all | bytes 524288 | tf_op jit(solution)/shard_map/all_to_all | solution.py:213
  18.8 0.7 %convert_reduce_fusion = f32[32,512]{1,0:T(8,128)} fusion(bf16[8,32,512]{2,1,0:T(8,128)(2,1)S(1)} %all_to_all.5), kind=kLoop, calls=%fused_computation | loop fusion | flops 245760 | bytes 327680 | tf_op jit(solution)/shard_map/reduce_sum | solution.py:214
Async XLA Ops:
  0.0 5.3 %collective-permute-start.1 = (bf16[3,2,512]{2,1,0:T(2,128)(2,1)}, bf16[3,2,512]{2,1,0:T(2,128)(2,1)S(1)}, u32[]{:S(2)}, u32[]{:S(2)}) collective-permute-start(bf16[3,2,512]{2,1,0:T(2,128)(2,1)} %bitcast.3), channel_id=1, source_target_pairs={{1,0},{2,1},{3,2},{4,3},{5,8},{6,5},{7,6},{8,7},{9,12},{10,9},{11,... | collective-permute-start | bytes 18440 | tf_op jit(solution)/shard_map/ppermute | solution.py:209
  2.2 3.1 %collective-permute-start = (bf16[3,2,512]{2,1,0:T(2,128)(2,1)}, bf16[3,2,512]{2,1,0:T(2,128)(2,1)S(1)}, u32[]{:S(2)}, u32[]{:S(2)}) collective-permute-start(bf16[3,2,512]{2,1,0:T(2,128)(2,1)} %bitcast.4), channel_id=1, source_target_pairs={{0,1},{1,0},{2,3},{3,2},{4,5},{5,4},{6,7},{7,6},{8,9},{9,8},{10,11... | collective-permute-start | bytes 18440 | tf_op jit(solution)/shard_map/ppermute | solution.py:209

commit v10 on v9

--- a/solution.py
+++ b/solution.py
@@ -114,7 +114,7 @@
     kcount, taps = placed_ref.shape[1:]
     count = block // LANES
     place = lax.axis_index("tm")
-    near = (place % 4 == 0).astype(jnp.float32)
+    near = (place % 4 == 2).astype(jnp.float32)
     far = (1.0 - near) * (place < lax.axis_size("tm") - 1).astype(jnp.float32)
     arrived = zip(backwards(chip_ref, range(count)), backwards(next_ref, range(count)))
     rows = jnp.concatenate([chip * near + other * far for chip, other in arrived] + [tail_ref[...]], axis=1)
@@ -196,8 +196,8 @@
 
 def backward(count):
     pairs = {i: i - 1 for i in range(1, count)}
-    pairs.update({i: i + 3 for i in range(5, count - 3, 4)})
-    pairs.update({0: 4, count - 3: count - 1})
+    pairs.update({i: i + 3 for i in range(3, count - 5, 4)})
+    pairs.update({0: 2, count - 5: count - 1})
     return list(pairs.items())
 
 

time: 19.6 us -> 20.4 us (1.041)
  the two profiles are of different devices: /device:TPU:96 before, /device:TPU:113 now
where the time goes in v10:
time: 20.4 us; the launch traced here: 20.1 us
  blocking collectives  11.5 us (56%)
  starting transfers between devices  3.41 us (17%)
  Pallas kernels  3.08 us (15%)
  waiting for transfers between devices  1.4 us (7%)
  other arithmetic  0.67 us (3%)
    all_to_all x1, blocking collectives, shards(): parts = lax.all_to_all(partial, 'sta', 0, 0)  11.5 us
    ppermute x1, starting transfers between devices, shards(): lax.ppermute(own, 'tm', backward(count))  3.41 us
    pallas_call x1, Pallas kernels, near_part(): pl.pallas_call(lambda *refs: near_kernel(*refs, gain=gain), out_shape=[ja...  2.06 us
    ppermute x1, waiting for transfers between devices, shards(): lax.ppermute(own, 'tm', backward(count))  1.4 us
    pallas_call x1, Pallas kernels, stack_part(): pl.pallas_call(stack_kernel, out_shape=jax.ShapeDtypeStruct((groups, kcou...  1.02 us
    reduce_sum x1, other arithmetic, shards(): return jnp.sum(parts.astype(jnp.float32), axis=0)  0.67 us
  transfers between devices with their start and end apart: 2, of which 1 were waited for; matrix products, arithmetic and copies ran while one was open for 0% of the time, Pallas kernels for 10%

profile of v10, /device:TPU:113, one launch (start us, length us, event | category | flops | bytes accessed | tf_op | source)
XLA Modules:
  0.0 20.1 jit_solution(13271797684771520259)
XLA Ops:
  0.0 3.4 %collective-permute-start.1 = (bf16[3,2,512]{2,1,0:T(2,128)(2,1)}, bf16[3,2,512]{2,1,0:T(2,128)(2,1)S(1)}, u32[]{:S(2)}, u32[]{:S(2)}) collective-permute-start(bf16[3,2,512]{2,1,0:T(2,128)(2,1)} %bitcast.3), channel_id=1, source_target_pairs={{1,0},{2,1},{3,6},{4,3},{5,4},{6,5},{7,10},{8,7},{9,8},{10,9},{11,... | collective-permute-start | bytes 18440 | tf_op jit(solution)/shard_map/ppermute | solution.py:209
  3.4 0.0 collective-permute-start
  3.4 2.1 %near.1 = (bf16[2,256,768]{2,1,0:T(8,128)(2,1)S(1)}, f32[8,256]{1,0:T(8,128)S(1)}, f32[2,8,128]{2,1,0:T(8,128)S(1)}, f32[2,256,128]{2,1,0:T(8,128)S(1)}, s32[2,2...) custom-call(s32[1,2]{1,0:T(1,128)} %bitcast.7, ...), custom_call_target="tpu_custom_call" | custom-call | tf_op jit(solution)/shard_map/near/pallas_call | solution.py:156
  5.5 1.4 %collective-permute-done.1.next_ref = bf16[3,2,512]{2,1,0:T(2,128)(2,1)S(1)} collective-permute-done((bf16[3,2,512]{2,1,0:T(2,128)(2,1)}, bf16[3,2,512]{2,1,0:T(2,128)(2,1)S(1)}, u32[]{:S(2)}, u32[]{:S(2)}) %collective-permute-start.1) | collective-permute-done | bytes 6176 | tf_op jit(solution)/shard_map/ppermute | solution.py:209
  6.9 0.0 collective-permute-done.chip_ref
  6.9 1.0 %stack.1 = bf16[8,32,512]{2,1,0:T(8,128)(2,1)S(1)} custom-call(bf16[3,2,512]{2,1,0:T(2,128)(2,1)S(1)} %collective-permute-done.chip_ref, bf16[3,2,512]{2,1,0:T(2,128)(2,1)S(1)} %collective-permute-done.1.next_ref, bf16[2,256,768]{2,1,0:T(8,128)(2,1)S(1)} %get-tuple-element.13.placed_ref, f32[8,256]{1,0:T(8,128)S(1)} %get-tuple-element.14.tail_ref, ...), custom_call_target="tpu_custom_call" | custom-call | tf_op jit(solution)/shard_map/stack/pallas_call | solution.py:182
  7.9 11.5 %all_to_all.5 = bf16[8,32,512]{2,1,0:T(8,128)(2,1)S(1)} all-to-all(bf16[8,32,512]{2,1,0:T(8,128)(2,1)S(1)} %stack.1), channel_id=1, replica_groups=mesh['sta'=8,'tm'=32] {'sta'}, dimensions={0} | all-to-all | bytes 524288 | tf_op jit(solution)/shard_map/all_to_all | solution.py:213
  19.4 0.7 %convert_reduce_fusion = f32[32,512]{1,0:T(8,128)} fusion(bf16[8,32,512]{2,1,0:T(8,128)(2,1)S(1)} %all_to_all.5), kind=kLoop, calls=%fused_computation | loop fusion | flops 245760 | bytes 327680 | tf_op jit(solution)/shard_map/reduce_sum | solution.py:214
Async XLA Ops:
  0.0 6.9 %collective-permute-start.1 = (bf16[3,2,512]{2,1,0:T(2,128)(2,1)}, bf16[3,2,512]{2,1,0:T(2,128)(2,1)S(1)}, u32[]{:S(2)}, u32[]{:S(2)}) collective-permute-start(bf16[3,2,512]{2,1,0:T(2,128)(2,1)} %bitcast.3), channel_id=1, source_target_pairs={{1,0},{2,1},{3,6},{4,3},{5,4},{6,5},{7,10},{8,7},{9,8},{10,9},{11,... | collective-permute-start | bytes 18440 | tf_op jit(solution)/shard_map/ppermute | solution.py:209
  3.4 3.5 %collective-permute-start = (bf16[3,2,512]{2,1,0:T(2,128)(2,1)}, bf16[3,2,512]{2,1,0:T(2,128)(2,1)S(1)}, u32[]{:S(2)}, u32[]{:S(2)}) collective-permute-start(bf16[3,2,512]{2,1,0:T(2,128)(2,1)} %bitcast.4), channel_id=1, source_target_pairs={{0,1},{1,0},{2,3},{3,2},{4,5},{5,4},{6,7},{7,6},{8,9},{9,8},{10,11... | collective-permute-start | bytes 18440 | tf_op jit(solution)/shard_map/ppermute | solution.py:209

commit v11 on v9

--- a/solution.py
+++ b/solution.py
@@ -107,7 +107,7 @@
 
 
 def stack_kernel(
-    chip_ref, next_ref, placed_ref, tail_ref, factor_ref, scale_ref, delay_ref, corner_ref, joined_ref, turned_ref,
+    next_ref, chip_ref, placed_ref, tail_ref, factor_ref, scale_ref, delay_ref, corner_ref, joined_ref, turned_ref,
     out_ref, frames_ref
 ):
     components, stations, block = next_ref.shape
@@ -206,7 +206,7 @@
     count = lax.axis_size("tm")
     groups = lax.axis_size("sta")
     own = jnp.transpose(record, (1, 0, 2))
-    ahead = (lax.ppermute(own, "tm", swapped(count)), lax.ppermute(own, "tm", backward(count)))
+    ahead = (lax.ppermute(own, "tm", backward(count)), lax.ppermute(own, "tm", swapped(count)))
     gain = math.sqrt(components * TLEN / (stations * groups))
     near = near_part(own, templates, moveouts, live_mask, owner_order, gain)
     partial = stack_part(ahead, near, groups)

time: 19.6 us -> 20.2 us (1.031)
  the two profiles are of different devices: /device:TPU:96 before, /device:TPU:1 now
where the time goes in v11:
time: 20.2 us; the launch traced here: 20 us
  blocking collectives  10.3 us (51%)
  starting transfers between devices  3.24 us (16%)
  Pallas kernels  3.07 us (15%)
  waiting for transfers between devices  2.69 us (13%)
  other arithmetic  0.67 us (3%)
    all_to_all x1, blocking collectives, shards(): parts = lax.all_to_all(partial, 'sta', 0, 0)  10.3 us
    ppermute x1, starting transfers between devices, shards(): lax.ppermute(own, 'tm', swapped(count))  3.24 us
    ppermute x1, waiting for transfers between devices, shards(): lax.ppermute(own, 'tm', backward(count))  2.69 us
    pallas_call x1, Pallas kernels, near_part(): pl.pallas_call(lambda *refs: near_kernel(*refs, gain=gain), out_shape=[ja...  2.06 us
    pallas_call x1, Pallas kernels, stack_part(): pl.pallas_call(stack_kernel, out_shape=jax.ShapeDtypeStruct((groups, kcou...  1.01 us
    reduce_sum x1, other arithmetic, shards(): return jnp.sum(parts.astype(jnp.float32), axis=0)  0.67 us
  transfers between devices with their start and end apart: 2, of which 1 were waited for; matrix products, arithmetic and copies ran while one was open for 0% of the time, Pallas kernels for 10%

profile of v11, /device:TPU:1, one launch (start us, length us, event | category | flops | bytes accessed | tf_op | source)
XLA Modules:
  0.0 20.0 jit_solution(1297647051064078477)
XLA Ops:
  0.0 3.2 %collective-permute-start.1 = (bf16[3,2,512]{2,1,0:T(2,128)(2,1)}, bf16[3,2,512]{2,1,0:T(2,128)(2,1)S(1)}, u32[]{:S(2)}, u32[]{:S(2)}) collective-permute-start(bf16[3,2,512]{2,1,0:T(2,128)(2,1)} %bitcast.3), channel_id=1, source_target_pairs={{0,1},{1,0},{2,3},{3,2},{4,5},{5,4},{6,7},{7,6},{8,9},{9,8},{10,11... | collective-permute-start | bytes 18440 | tf_op jit(solution)/shard_map/ppermute | solution.py:209
  3.2 0.0 collective-permute-start
  3.2 2.1 %near.1 = (bf16[2,256,768]{2,1,0:T(8,128)(2,1)S(1)}, f32[8,256]{1,0:T(8,128)S(1)}, f32[2,8,128]{2,1,0:T(8,128)S(1)}, f32[2,256,128]{2,1,0:T(8,128)S(1)}, s32[2,2...) custom-call(s32[1,2]{1,0:T(1,128)} %bitcast.7, ...), custom_call_target="tpu_custom_call" | custom-call | tf_op jit(solution)/shard_map/near/pallas_call | solution.py:156
  5.3 0.0 collective-permute-done.1.chip_ref
  5.3 2.7 %collective-permute-done.next_ref = bf16[3,2,512]{2,1,0:T(2,128)(2,1)S(1)} collective-permute-done((bf16[3,2,512]{2,1,0:T(2,128)(2,1)}, bf16[3,2,512]{2,1,0:T(2,128)(2,1)S(1)}, u32[]{:S(2)}, u32[]{:S(2)}) %collective-permute-start) | collective-permute-done | bytes 6176 | tf_op jit(solution)/shard_map/ppermute | solution.py:209
  8.0 1.0 %stack.1 = bf16[8,32,512]{2,1,0:T(8,128)(2,1)S(1)} custom-call(bf16[3,2,512]{2,1,0:T(2,128)(2,1)S(1)} %collective-permute-done.next_ref, bf16[3,2,512]{2,1,0:T(2,128)(2,1)S(1)} %collective-permute-done.1.chip_ref, bf16[2,256,768]{2,1,0:T(8,128)(2,1)S(1)} %get-tuple-element.13.placed_ref, f32[8,256]{1,0:T(8,128)S(1)} %get-tuple-element.14.tail_ref, ...), custom_call_target="tpu_custom_call" | custom-call | tf_op jit(solution)/shard_map/stack/pallas_call | solution.py:182
  9.0 10.3 %all_to_all.5 = bf16[8,32,512]{2,1,0:T(8,128)(2,1)S(1)} all-to-all(bf16[8,32,512]{2,1,0:T(8,128)(2,1)S(1)} %stack.1), channel_id=1, replica_groups=mesh['sta'=8,'tm'=32] {'sta'}, dimensions={0} | all-to-all | bytes 524288 | tf_op jit(solution)/shard_map/all_to_all | solution.py:213
  19.3 0.7 %convert_reduce_fusion = f32[32,512]{1,0:T(8,128)} fusion(bf16[8,32,512]{2,1,0:T(8,128)(2,1)S(1)} %all_to_all.5), kind=kLoop, calls=%fused_computation | loop fusion | flops 245760 | bytes 327680 | tf_op jit(solution)/shard_map/reduce_sum | solution.py:214
Async XLA Ops:
  0.0 5.3 %collective-permute-start.1 = (bf16[3,2,512]{2,1,0:T(2,128)(2,1)}, bf16[3,2,512]{2,1,0:T(2,128)(2,1)S(1)}, u32[]{:S(2)}, u32[]{:S(2)}) collective-permute-start(bf16[3,2,512]{2,1,0:T(2,128)(2,1)} %bitcast.3), channel_id=1, source_target_pairs={{0,1},{1,0},{2,3},{3,2},{4,5},{5,4},{6,7},{7,6},{8,9},{9,8},{10,11... | collective-permute-start | bytes 18440 | tf_op jit(solution)/shard_map/ppermute | solution.py:209
  3.2 4.8 %collective-permute-start = (bf16[3,2,512]{2,1,0:T(2,128)(2,1)}, bf16[3,2,512]{2,1,0:T(2,128)(2,1)S(1)}, u32[]{:S(2)}, u32[]{:S(2)}) collective-permute-start(bf16[3,2,512]{2,1,0:T(2,128)(2,1)} %bitcast.4), channel_id=1, source_target_pairs={{1,0},{2,1},{3,2},{4,3},{5,8},{6,5},{7,6},{8,7},{9,12},{10,9},{11,... | collective-permute-start | bytes 18440 | tf_op jit(solution)/shard_map/ppermute | solution.py:209

commit v12 on v9

--- a/solution.py
+++ b/solution.py
@@ -108,7 +108,7 @@
 
 def stack_kernel(
     chip_ref, next_ref, placed_ref, tail_ref, factor_ref, scale_ref, delay_ref, corner_ref, joined_ref, turned_ref,
-    out_ref, frames_ref
+    out_ref
 ):
     components, stations, block = next_ref.shape
     kcount, taps = placed_ref.shape[1:]
@@ -120,16 +120,14 @@
     rows = jnp.concatenate([chip * near + other * far for chip, other in arrived] + [tail_ref[...]], axis=1)
     total = [jnp.zeros((kcount, LANES), jnp.float32) for _ in range(count)]
     for s in range(stations):
+        record_scale = record_scale_of(rows, stations, s, taps)
+        frames = []
         for c in range(components):
             r = c * stations + s
             steps = staircase(rows[r : r + 1, : (count + 1) * LANES], LANES, 1).astype(jnp.bfloat16)
-            start = c * TLEN
-            frames_ref[s, start : start + LANES, : (count - 1) * LANES] = steps[:, 2 * LANES :]
-            frames_ref[s, start : start + LANES, (count - 1) * LANES :] = corner_ref[s, c * LANES : (c + 1) * LANES, :]
-            frames_ref[s, start + LANES : start + TLEN, :] = steps[:, LANES:]
-    for s in range(stations):
-        record_scale = record_scale_of(rows, stations, s, taps)
-        correlation = jnp.dot(placed_ref[s], frames_ref[s], preferred_element_type=jnp.float32)
+            corner = corner_ref[s, c * LANES : (c + 1) * LANES, :]
+            frames += [jnp.concatenate([steps[:, 2 * LANES :], corner], axis=1), steps[:, LANES:]]
+        correlation = jnp.dot(placed_ref[s], jnp.concatenate(frames, axis=0), preferred_element_type=jnp.float32)
         moveout = delay_ref[s]
         reach = lag(moveout)
         far = moveout >= LANES
@@ -184,7 +182,6 @@
         out_shape=jax.ShapeDtypeStruct((groups, kcount // groups, block), jnp.bfloat16),
         in_specs=[vmem] * (len(ahead) + len(near)),
         out_specs=vmem,
-        scratch_shapes=[pltpu.VMEM((stations, taps, block), jnp.bfloat16)],
         compiler_params=pltpu.CompilerParams(vmem_limit_bytes=32 << 20),
         name="stack",
     )(*ahead, *near)

time: 19.6 us -> 19.6 us (level)
  no operation moved by 1% of the time
where the time goes in v12:
time: 19.6 us; the launch traced here: 19.4 us
  blocking collectives  12.4 us (63%)
  starting transfers between devices  3.24 us (17%)
  Pallas kernels  3.07 us (16%)
  other arithmetic  0.67 us (3%)
    all_to_all x1, blocking collectives, shards(): parts = lax.all_to_all(partial, 'sta', 0, 0)  12.4 us
    ppermute x1, starting transfers between devices, shards(): lax.ppermute(own, 'tm', backward(count))  2.18 us
    pallas_call x1, Pallas kernels, near_part(): pl.pallas_call(lambda *refs: near_kernel(*refs, gain=gain), out_shape=[ja...  2.06 us
    ppermute x1, starting transfers between devices, shards(): lax.ppermute(own, 'tm', swapped(count))  1.06 us
    pallas_call x1, Pallas kernels, stack_part(): pl.pallas_call(stack_kernel, out_shape=jax.ShapeDtypeStruct((groups, kcou...  1.01 us
    reduce_sum x1, other arithmetic, shards(): return jnp.sum(parts.astype(jnp.float32), axis=0)  0.67 us
  transfers between devices with their start and end apart: 2, of which 0 were waited for; matrix products, arithmetic and copies ran while one was open for 0% of the time, Pallas kernels for 11%

profile of v12, /device:TPU:96, one launch (start us, length us, event | category | flops | bytes accessed | tf_op | source)
XLA Modules:
  0.0 19.4 jit_solution(18398338784005342559)
XLA Ops:
  0.0 2.2 %collective-permute-start.1 = (bf16[3,2,512]{2,1,0:T(2,128)(2,1)}, bf16[3,2,512]{2,1,0:T(2,128)(2,1)S(1)}, u32[]{:S(2)}, u32[]{:S(2)}) collective-permute-start(bf16[3,2,512]{2,1,0:T(2,128)(2,1)} %bitcast.3), channel_id=1, source_target_pairs={{1,0},{2,1},{3,2},{4,3},{5,8},{6,5},{7,6},{8,7},{9,12},{10,9},{11,... | collective-permute-start | bytes 18440 | tf_op jit(solution)/shard_map/ppermute | solution.py:206
  2.2 1.1 %collective-permute-start = (bf16[3,2,512]{2,1,0:T(2,128)(2,1)}, bf16[3,2,512]{2,1,0:T(2,128)(2,1)S(1)}, u32[]{:S(2)}, u32[]{:S(2)}) collective-permute-start(bf16[3,2,512]{2,1,0:T(2,128)(2,1)} %bitcast.4), channel_id=1, source_target_pairs={{0,1},{1,0},{2,3},{3,2},{4,5},{5,4},{6,7},{7,6},{8,9},{9,8},{10,11... | collective-permute-start | bytes 18440 | tf_op jit(solution)/shard_map/ppermute | solution.py:206
  3.2 2.1 %near.1 = (bf16[2,256,768]{2,1,0:T(8,128)(2,1)S(1)}, f32[8,256]{1,0:T(8,128)S(1)}, f32[2,8,128]{2,1,0:T(8,128)S(1)}, f32[2,256,128]{2,1,0:T(8,128)S(1)}, s32[2,2...) custom-call(s32[1,2]{1,0:T(1,128)} %bitcast.7, ...), custom_call_target="tpu_custom_call" | custom-call | tf_op jit(solution)/shard_map/near/pallas_call | solution.py:154
  5.3 0.0 collective-permute-done.1.next_ref
  5.3 0.0 collective-permute-done.chip_ref
  5.3 1.0 %stack.1 = bf16[8,32,512]{2,1,0:T(8,128)(2,1)S(1)} custom-call(bf16[3,2,512]{2,1,0:T(2,128)(2,1)S(1)} %collective-permute-done.chip_ref, bf16[3,2,512]{2,1,0:T(2,128)(2,1)S(1)} %collective-permute-done.1.next_ref, bf16[2,256,768]{2,1,0:T(8,128)(2,1)S(1)} %get-tuple-element.13.placed_ref, f32[8,256]{1,0:T(8,128)S(1)} %get-tuple-element.14.tail_ref, ...), custom_call_target="tpu_custom_call" | custom-call | tf_op jit(solution)/shard_map/stack/pallas_call | solution.py:180
  6.3 12.4 %all_to_all.5 = bf16[8,32,512]{2,1,0:T(8,128)(2,1)S(1)} all-to-all(bf16[8,32,512]{2,1,0:T(8,128)(2,1)S(1)} %stack.1), channel_id=1, replica_groups=mesh['sta'=8,'tm'=32] {'sta'}, dimensions={0} | all-to-all | bytes 524288 | tf_op jit(solution)/shard_map/all_to_all | solution.py:210
  18.7 0.7 %convert_reduce_fusion = f32[32,512]{1,0:T(8,128)} fusion(bf16[8,32,512]{2,1,0:T(8,128)(2,1)S(1)} %all_to_all.5), kind=kLoop, calls=%fused_computation | loop fusion | flops 245760 | bytes 327680 | tf_op jit(solution)/shard_map/reduce_sum | solution.py:211
Async XLA Ops:
  0.0 5.3 %collective-permute-start.1 = (bf16[3,2,512]{2,1,0:T(2,128)(2,1)}, bf16[3,2,512]{2,1,0:T(2,128)(2,1)S(1)}, u32[]{:S(2)}, u32[]{:S(2)}) collective-permute-start(bf16[3,2,512]{2,1,0:T(2,128)(2,1)} %bitcast.3), channel_id=1, source_target_pairs={{1,0},{2,1},{3,2},{4,3},{5,8},{6,5},{7,6},{8,7},{9,12},{10,9},{11,... | collective-permute-start | bytes 18440 | tf_op jit(solution)/shard_map/ppermute | solution.py:206
  2.2 3.1 %collective-permute-start = (bf16[3,2,512]{2,1,0:T(2,128)(2,1)}, bf16[3,2,512]{2,1,0:T(2,128)(2,1)S(1)}, u32[]{:S(2)}, u32[]{:S(2)}) collective-permute-start(bf16[3,2,512]{2,1,0:T(2,128)(2,1)} %bitcast.4), channel_id=1, source_target_pairs={{0,1},{1,0},{2,3},{3,2},{4,5},{5,4},{6,7},{7,6},{8,9},{9,8},{10,11... | collective-permute-start | bytes 18440 | tf_op jit(solution)/shard_map/ppermute | solution.py:206

commit v13 on v9

--- a/solution.py
+++ b/solution.py
@@ -91,14 +91,16 @@
     for s in range(stations):
         delay_ref[s] = jnp.broadcast_to(delays[:, s : s + 1], (kcount, LANES))
         factor_ref[s] = jnp.broadcast_to(live_ref[0:1, s : s + 1].astype(jnp.float32) * gain, (8, LANES))
+    wides = [jnp.dot(chosen, template_ref[s], preferred_element_type=jnp.float32) for s in range(stations)]
     for s in range(stations):
         record_scale = record_scale_of(rows, stations, s, taps)
-        wide = jnp.dot(chosen, template_ref[s], preferred_element_type=jnp.float32)
-        placed_ref[s] = wide.astype(jnp.bfloat16)
+        wide = wides[s]
+        placed = wide.astype(jnp.bfloat16)
+        placed_ref[s] = placed
         energy = jnp.sum(wide * wide, axis=1, keepdims=True)
         scale = jnp.broadcast_to(1.0 / jnp.sqrt(energy / taps + epsilon), (kcount, LANES))
         scale_ref[s] = scale
-        correlation = jnp.dot(placed_ref[s], frames_ref[s], preferred_element_type=jnp.float32)
+        correlation = jnp.dot(placed, frames_ref[s], preferred_element_type=jnp.float32)
         reach = lag(delay_ref[s])
         first = turn(block_of(correlation, 1), block_of(record_scale, last), scale, reach)
         second = turn(block_of(correlation, 0), block_of(record_scale, last - 1), scale, reach)

time: 19.6 us -> 19.6 us (level)
  transfers between devices with their start and end apart: 2 -> 2, of which waited for: 0 -> 0; matrix products, arithmetic and copies ran while one was open for 0% -> 0% of each run, Pallas kernels for 11% -> 10%
where the time goes in v13:
time: 19.6 us; the launch traced here: 19.4 us
  blocking collectives  12.4 us (63%)
  starting transfers between devices  3.24 us (17%)
  Pallas kernels  3.06 us (16%)
  other arithmetic  0.67 us (3%)
    all_to_all x1, blocking collectives, shards(): parts = lax.all_to_all(partial, 'sta', 0, 0)  12.4 us
    ppermute x1, starting transfers between devices, shards(): lax.ppermute(own, 'tm', backward(count))  2.18 us
    pallas_call x1, Pallas kernels, near_part(): pl.pallas_call(lambda *refs: near_kernel(*refs, gain=gain), out_shape=[ja...  2.04 us
    ppermute x1, starting transfers between devices, shards(): lax.ppermute(own, 'tm', swapped(count))  1.06 us
    pallas_call x1, Pallas kernels, stack_part(): pl.pallas_call(stack_kernel, out_shape=jax.ShapeDtypeStruct((groups, kcou...  1.02 us
    reduce_sum x1, other arithmetic, shards(): return jnp.sum(parts.astype(jnp.float32), axis=0)  0.67 us
  transfers between devices with their start and end apart: 2, of which 0 were waited for; matrix products, arithmetic and copies ran while one was open for 0% of the time, Pallas kernels for 10%

profile of v13, /device:TPU:96, one launch (start us, length us, event | category | flops | bytes accessed | tf_op | source)
XLA Modules:
  0.0 19.4 jit_solution(5890317081830707111)
XLA Ops:
  0.0 2.2 %collective-permute-start.1 = (bf16[3,2,512]{2,1,0:T(2,128)(2,1)}, bf16[3,2,512]{2,1,0:T(2,128)(2,1)S(1)}, u32[]{:S(2)}, u32[]{:S(2)}) collective-permute-start(bf16[3,2,512]{2,1,0:T(2,128)(2,1)} %bitcast.3), channel_id=1, source_target_pairs={{1,0},{2,1},{3,2},{4,3},{5,8},{6,5},{7,6},{8,7},{9,12},{10,9},{11,... | collective-permute-start | bytes 18440 | tf_op jit(solution)/shard_map/ppermute | solution.py:211
  2.2 1.1 %collective-permute-start = (bf16[3,2,512]{2,1,0:T(2,128)(2,1)}, bf16[3,2,512]{2,1,0:T(2,128)(2,1)S(1)}, u32[]{:S(2)}, u32[]{:S(2)}) collective-permute-start(bf16[3,2,512]{2,1,0:T(2,128)(2,1)} %bitcast.4), channel_id=1, source_target_pairs={{0,1},{1,0},{2,3},{3,2},{4,5},{5,4},{6,7},{7,6},{8,9},{9,8},{10,11... | collective-permute-start | bytes 18440 | tf_op jit(solution)/shard_map/ppermute | solution.py:211
  3.2 2.0 %near.1 = (bf16[2,256,768]{2,1,0:T(8,128)(2,1)S(1)}, f32[8,256]{1,0:T(8,128)S(1)}, f32[2,8,128]{2,1,0:T(8,128)S(1)}, f32[2,256,128]{2,1,0:T(8,128)S(1)}, s32[2,2...) custom-call(s32[1,2]{1,0:T(1,128)} %bitcast.7, ...), custom_call_target="tpu_custom_call" | custom-call | tf_op jit(solution)/shard_map/near/pallas_call | solution.py:158
  5.3 0.0 collective-permute-done.1.next_ref
  5.3 0.0 collective-permute-done.chip_ref
  5.3 1.0 %stack.1 = bf16[8,32,512]{2,1,0:T(8,128)(2,1)S(1)} custom-call(bf16[3,2,512]{2,1,0:T(2,128)(2,1)S(1)} %collective-permute-done.chip_ref, bf16[3,2,512]{2,1,0:T(2,128)(2,1)S(1)} %collective-permute-done.1.next_ref, bf16[2,256,768]{2,1,0:T(8,128)(2,1)S(1)} %get-tuple-element.13.placed_ref, f32[8,256]{1,0:T(8,128)S(1)} %get-tuple-element.14.tail_ref, ...), custom_call_target="tpu_custom_call" | custom-call | tf_op jit(solution)/shard_map/stack/pallas_call | solution.py:184
  6.3 12.4 %all_to_all.5 = bf16[8,32,512]{2,1,0:T(8,128)(2,1)S(1)} all-to-all(bf16[8,32,512]{2,1,0:T(8,128)(2,1)S(1)} %stack.1), channel_id=1, replica_groups=mesh['sta'=8,'tm'=32] {'sta'}, dimensions={0} | all-to-all | bytes 524288 | tf_op jit(solution)/shard_map/all_to_all | solution.py:215
  18.7 0.7 %convert_reduce_fusion = f32[32,512]{1,0:T(8,128)} fusion(bf16[8,32,512]{2,1,0:T(8,128)(2,1)S(1)} %all_to_all.5), kind=kLoop, calls=%fused_computation | loop fusion | flops 245760 | bytes 327680 | tf_op jit(solution)/shard_map/reduce_sum | solution.py:216
Async XLA Ops:
  0.0 5.3 %collective-permute-start.1 = (bf16[3,2,512]{2,1,0:T(2,128)(2,1)}, bf16[3,2,512]{2,1,0:T(2,128)(2,1)S(1)}, u32[]{:S(2)}, u32[]{:S(2)}) collective-permute-start(bf16[3,2,512]{2,1,0:T(2,128)(2,1)} %bitcast.3), channel_id=1, source_target_pairs={{1,0},{2,1},{3,2},{4,3},{5,8},{6,5},{7,6},{8,7},{9,12},{10,9},{11,... | collective-permute-start | bytes 18440 | tf_op jit(solution)/shard_map/ppermute | solution.py:211
  2.2 3.1 %collective-permute-start = (bf16[3,2,512]{2,1,0:T(2,128)(2,1)}, bf16[3,2,512]{2,1,0:T(2,128)(2,1)S(1)}, u32[]{:S(2)}, u32[]{:S(2)}) collective-permute-start(bf16[3,2,512]{2,1,0:T(2,128)(2,1)} %bitcast.4), channel_id=1, source_target_pairs={{0,1},{1,0},{2,3},{3,2},{4,5},{5,4},{6,7},{7,6},{8,9},{9,8},{10,11... | collective-permute-start | bytes 18440 | tf_op jit(solution)/shard_map/ppermute | solution.py:211
